TPU v7x, 128 devices: a whole 4x4x4 slice. The times are simulated.
128 devices in a mesh: row: 4 (over x_hi, core), col: 32 (over y, x_lo, z).
Axes of the slice: x: 4 (x_hi: 2, x_lo: 2; x = x_hi * 2 + x_lo), y: 4, z: 4, core: 2. Of those that a mesh axis runs over, the one named last changes fastest.
Arguments:
- tokens: bfloat16 [49152, 2048], P('col', 'row'), may hold values from -6 to 6
- in_weight: float32 [2048, 6144], P(('row', 'col')), may hold values from -0.125 to 0.125
- out_weight: float32 [2048, 2048], P(('row', 'col')), may hold values from -0.125 to 0.125
- beta_weight: float32 [2048, 16], replicated, may hold values from -0.25 to 0.25
- conv_weight: float32 [4, 6144], P(None, 'row'), may hold values from -2.5 to 2.5
- conv_prior: bfloat16 [96, 3, 6144], P('col', None, 'row'), may hold values from -6 to 6
- head_gain: float32 [2048], P('row'), may hold values from 0.1 to 1.9
- state_pool: float32 [192, 16, 128, 128], P('col', 'row'), may hold values from -2.5 to 2.5
- state_index: int32 [96, 16], P('col', 'row'), may hold values from 0 to 5
- lengths: int32 [96], P('col'), may hold values from 1 to 512, 36864 in all
- page_table: int32 [96, 4, 2], P('col'), may hold values from 0 to 31, as said below
Outputs:
- server_in: bfloat16 [2048, 6144], P('row', 'col')
- server_out: bfloat16 [2048, 2048], P('row', 'col')
- layer_out: bfloat16 [49152, 2048], P('col', 'row')
- final_state: float32 [96, 16, 128, 128], P('col', 'row')
- page_cache: bfloat16 [384, 128, 2, 2048], P('col', None, None, 'row')
Inputs may be any that keep to these rules, and one draw needn't show every extreme that they name: `lengths`: one prompt has all 512 tokens live. `state_index`: which of its own index of col's 6 stored states a prompt and head continues. page_table[p, g, 0] is the index of col that keeps page g of prompt p and page_table[p, g, 1] its slot there, below 12; every slot of every index of col gets exactly one page; the prompts of one index of col send at most 1 pages to any one index of col, and exactly 1 to some.
All inputs are finite; a program needn't handle non-finite values. No bound on the sum of `lengths` on one device may be relied on, other than what follows from the above.
Results may differ from a plain program's by a relative error of at most 0.029.
Values may be sent and summed in bfloat16 or wider, within the bound.
No kernel may reach another device: no remote copies, remote signals or barrier semaphores. Data moves between devices by JAX's collectives and lax.ppermute only.
A program may use at most 128 MiB of HBM per device.

v0:
```python
import jax
import jax.numpy as jnp
from jax import lax
from jax.sharding import PartitionSpec as P

DK = 128
STRETCH = 64
CONV = 4
SEQ = 512
PAGE = 128
PAGES_SEQ = 4


HIGHEST = lax.Precision.HIGHEST


def delta_block(carry_state, block_data):
    query_unit, key_unit, values, beta_rates = block_data
    width_c = beta_rates.shape[1]
    width_k = key_unit.shape[2]
    strict_lower = jnp.tril(jnp.ones((width_c, width_c), jnp.float32), -1)
    causal = jnp.tril(jnp.ones((width_c, width_c), jnp.float32))
    gram_matrix = jnp.einsum("bik,bjk->bij", key_unit, key_unit, precision=HIGHEST)
    system = (
        jnp.eye(width_c, dtype=jnp.float32) + beta_rates[:, :, None] * gram_matrix * strict_lower
    )
    right_side = jnp.concatenate([key_unit, values], axis=2) * beta_rates[:, :, None]
    solved = jax.scipy.linalg.solve_triangular(system, right_side, lower=True, unit_diagonal=True)
    weighted = solved[:, :, :width_k]
    corrected = solved[:, :, width_k:] - jnp.einsum(
        "bck,bkv->bcv", weighted, carry_state, precision=HIGHEST
    )
    scores = jnp.einsum("bik,bjk->bij", query_unit, key_unit, precision=HIGHEST) * causal
    output = jnp.einsum("bck,bkv->bcv", query_unit, carry_state, precision=HIGHEST) + jnp.einsum(
        "bij,bjv->biv", scores, corrected, precision=HIGHEST
    )
    carry_state = carry_state + jnp.einsum("bck,bcv->bkv", key_unit, corrected, precision=HIGHEST)
    return (carry_state, output)


def delta_scan(query_unit, key_unit, values, beta_rates, initial, block_len):
    batch_n = query_unit.shape[0]
    length_all = query_unit.shape[1]
    num_blocks = length_all // block_len

    def to_blocks(tensor):
        shaped = tensor.reshape((batch_n, num_blocks, block_len) + tensor.shape[2:])
        return jnp.moveaxis(shaped, 1, 0)

    last_state, outputs = lax.scan(
        delta_block,
        initial,
        (to_blocks(query_unit), to_blocks(key_unit), to_blocks(values), to_blocks(beta_rates)),
    )
    outputs = jnp.moveaxis(outputs, 0, 1).reshape(batch_n, length_all, -1)
    return (last_state, outputs)


def unit_rows(tensor):
    return tensor * lax.rsqrt(jnp.sum(tensor * tensor, axis=-1, keepdims=True) + 1e-06)


def local(
    tokens,
    in_weight,
    out_weight,
    beta_weight,
    conv_weight,
    conv_prior,
    head_gain,
    state_pool,
    state_index,
    lengths,
    page_table,
):
    row_count = lax.axis_size("row")
    col_count = lax.axis_size("col")
    row_id = lax.axis_index("row")
    local_tokens = tokens.shape[0]
    feature_span = tokens.shape[1]
    head_group = state_index.shape[1]
    head_width = 3 * DK
    prompts_here = lengths.shape[0]
    trainer_in = in_weight.astype(jnp.bfloat16)
    server_in, server_out = (
        lax.all_to_all(trainer_in, "col", split_axis=1, concat_axis=0, tiled=True),
        lax.all_to_all(
            out_weight.astype(jnp.bfloat16), "col", split_axis=1, concat_axis=0, tiled=True
        ),
    )
    beta_cast = beta_weight.astype(jnp.bfloat16)
    wide_in, wide_out = (
        lax.all_gather(server_in, "col", axis=1, tiled=True),
        lax.all_gather(server_out, "col", axis=1, tiled=True),
    )
    columns = wide_in
    product = jnp.dot(tokens, columns, preferred_element_type=jnp.float32)
    qkv_sum = lax.psum_scatter(
        product.reshape(local_tokens, lax.axis_size("row") * head_group, head_width)
        .transpose(1, 0, 2)
        .astype(jnp.bfloat16),
        "row",
        scatter_dimension=0,
        tiled=True,
    )
    beta_rows = lax.dynamic_slice_in_dim(beta_cast, row_id * feature_span, feature_span, 0)
    beta_term = jnp.dot(tokens, beta_rows, preferred_element_type=jnp.float32).T
    beta_sum = lax.psum_scatter(
        beta_term.astype(jnp.bfloat16), "row", scatter_dimension=0, tiled=True
    ).astype(jnp.float32)
    projected = qkv_sum.reshape(head_group, prompts_here, SEQ, head_width)
    prior_rows = conv_prior.reshape(prompts_here, CONV - 1, head_group, head_width).transpose(
        2, 0, 1, 3
    )
    padded = jnp.concatenate(
        [prior_rows.astype(jnp.float32), projected.astype(jnp.float32)], axis=2
    )
    taps_all = conv_weight.reshape(CONV, head_group, head_width)
    conv_sum = jnp.zeros(projected.shape, jnp.float32)
    for tap_id in range(CONV):
        conv_sum = (
            conv_sum + taps_all[tap_id][:, None, None, :] * padded[:, :, tap_id : tap_id + SEQ]
        )
    activated = jax.nn.silu(conv_sum).reshape(head_group * prompts_here, SEQ, 3, DK)
    query_unit = unit_rows(activated[:, :, 0])
    key_unit = unit_rows(activated[:, :, 1])
    values = activated[:, :, 2]
    live_mask = (jnp.arange(SEQ, dtype=jnp.int32)[None, :] < lengths[:, None]).astype(jnp.float32)
    live_batch = jnp.broadcast_to(live_mask[None], (head_group, prompts_here, SEQ)).reshape(
        head_group * prompts_here, SEQ
    )
    beta_rates = live_batch * jax.nn.sigmoid(beta_sum.reshape(head_group * prompts_here, SEQ))
    picked = state_pool[state_index, jnp.arange(head_group, dtype=jnp.int32)[None, :]]
    initial = picked.transpose(1, 0, 2, 3).reshape(head_group * prompts_here, DK, DK)
    last_state, outputs = delta_scan(query_unit, key_unit, values, beta_rates, initial, STRETCH)
    outputs = outputs * live_batch[:, :, None]
    normed = outputs.reshape(head_group, prompts_here, SEQ, DK)
    normed = (
        normed
        * lax.rsqrt(jnp.mean(normed * normed, axis=3, keepdims=True) + 1e-05)
        * head_gain.reshape(head_group, 1, 1, DK)
    )
    flat_heads = (
        normed.astype(jnp.bfloat16).transpose(1, 2, 0, 3).reshape(local_tokens, head_group * DK)
    )
    out_span = wide_out.shape[1] // row_count
    columns = wide_out
    product = jnp.dot(flat_heads, columns, preferred_element_type=jnp.float32)
    layer_out = (
        lax.psum_scatter(
            product.reshape(local_tokens, lax.axis_size("row") * 1, out_span)
            .transpose(1, 0, 2)
            .astype(jnp.bfloat16),
            "row",
            scatter_dimension=0,
            tiled=True,
        )
        .astype(jnp.float32)[0]
        .astype(jnp.bfloat16)
    )
    final_state = last_state.reshape(head_group, prompts_here, DK, DK).transpose(1, 0, 2, 3)
    keep_mask = live_batch[:, :, None]
    kept_pairs = jnp.stack([key_unit * keep_mask, values * keep_mask], axis=0).reshape(
        2, head_group, prompts_here, SEQ, DK
    )
    page_rows = (
        kept_pairs.transpose(2, 3, 0, 1, 4)
        .reshape(prompts_here * PAGES_SEQ, PAGE, 2, head_group * DK)
        .astype(jnp.bfloat16)
    )
    pages_dev = page_rows.shape[0]
    capacity = max(1, 2 * pages_dev // col_count)
    targets = page_table[:, :, 0].reshape(-1)
    slot_ids = page_table[:, :, 1].reshape(-1)
    order_ids = jnp.arange(pages_dev, dtype=jnp.int32)
    earlier = (targets[:, None] == targets[None, :]) & (order_ids[None, :] < order_ids[:, None])
    positions = targets * capacity + jnp.sum(earlier.astype(jnp.int32), axis=1)
    outgoing = (
        jnp.zeros((col_count * capacity,) + page_rows.shape[1:], jnp.bfloat16)
        .at[positions]
        .set(page_rows)
    )
    slot_send = jnp.full((col_count * capacity,), pages_dev, jnp.int32).at[positions].set(slot_ids)
    arrived, arrived_slots = (
        lax.all_to_all(outgoing, "col", split_axis=0, concat_axis=0, tiled=True),
        lax.all_to_all(slot_send, "col", split_axis=0, concat_axis=0, tiled=True),
    )
    page_cache = (
        jnp.zeros(page_rows.shape, jnp.bfloat16).at[arrived_slots].set(arrived, mode="drop")
    )
    return (server_in, server_out, layer_out, final_state, page_cache)


def solution(mesh):
    return jax.shard_map(
        local,
        mesh=mesh,
        in_specs=(
            P("col", "row"),
            P(("row", "col"), None),
            P(("row", "col"), None),
            P(),
            P(None, "row"),
            P("col", None, "row"),
            P("row"),
            P("col", "row", None, None),
            P("col", "row"),
            P("col"),
            P("col", None, None),
        ),
        out_specs=(
            P("row", "col"),
            P("row", "col"),
            P("col", "row"),
            P("col", "row", None, None),
            P("col", None, None, "row"),
        ),
        check_vma=False,
    )
```

profile of v0, /device:TPU:16, one launch (start us, length us, event | category | flops | bytes accessed | tf_op | source)
XLA Modules:
  0.0 1225.6 jit_solution(3627169898886624098)
XLA Ops:
  8.8 16.4 %all_to_all.55 = bf16[16,32,192]{2,0,1:T(8,128)(2,1)S(1)} all-to-all(bf16[16,32,192]{2,0,1:T(8,128)(2,1)S(1)} %copy.123), channel_id=1, replica_groups=mesh['row'=4,'col'=32] {'col'}, dimensions={1} | all-to-all | bytes 393216 | tf_op jit(solution)/shard_map/all_to_all | solution.py:86
  26.1 144.7 %all-gather.3.cloned.1.call-done = bf16[512,6144]{0,1:T(8,128)(2,1)} async-done(((bf16[512,192]{0,1:T(8,128)(2,1)}), bf16[512,6144]{0,1:T(8,128)(2,1)}) %all-gather.3.cloned.1.call-update) | async-done | bytes 6291472 | tf_op jit(solution)/shard_map/all_gather | solution.py:93
  170.8 15.9 %convolution_convert_fusion = bf16[1536,6144]{1,0:T(8,128)(2,1)} fusion(bf16[1536,512]{1,0:T(8,128)(2,1)S(1)} %copy-done, bf16[512,6144]{0,1:T(8,128)(2,1)} %all-gather.3.cloned.1.call-done), kind=kOutput, calls=%fused_computation.43 | convolution fusion | flops 9673113600 | bytes 26738688 | tf_op jit(solution)/shard_map/dot_general | solution.py:97
  186.7 18.3 %copy.164 = bf16[192,16,8,384]{3,2,0,1:T(8,128)(2,1)} copy(bf16[192,16,8,384]{3,2,1,0:T(8,128)(2,1)} %bitcast.161) | data formatting | bytes 37748736 | tf_op jit(solution)/shard_map/convert_element_type | solution.py:101
  207.0 25.2 %all-to-all-start.1 = ((bf16[32,2,512]{2,1,0:T(2,128)(2,1)}), bf16[32,2,512]{2,1,0:T(2,128)(2,1)S(1)}, u32[]{:S(2)}, u32[]{:S(2)}) async-start(bf16[32,2,512]{2,1,0:T(2,128)(2,1)} %reshape.338), calls=%async_computation.1 | async-start | bytes 131072 | tf_op jit(solution)/shard_map/all_to_all | solution.py:87
  234.8 13.6 %all-reduce = bf16[16,1536]{1,0:T(8,128)(2,1)S(1)} all-reduce(bf16[16,1536]{1,0:T(8,128)(2,1)S(1)} %convolution_convert_fusion.1), channel_id=3, replica_groups=mesh['row'=4,'col'=32] {'row'}, use_global_device_ids=true, to_apply=%region_3.4.clone | all-reduce | flops 24576 | bytes 98304
  252.5 116.9 %reduce-scatter.3.cloned.1.call-done = bf16[4,1536,384]{2,1,0:T(8,128)(2,1)} async-done(((bf16[16,1536,384]{2,1,0:T(8,128)(2,1)}), bf16[4,1536,384]{2,1,0:T(8,128)(2,1)}) %reduce-scatter.3.cloned.1.call-update) | async-done | bytes 4718608 | tf_op jit(solution)/shard_map/reduce_scatter | solution.py:98
  372.6 7.4 divide_multiply_fusion
  380.0 9.7 copy.129
  389.6 8.1 multiply_reduce_fusion
  414.5 554.7 %while.12 = (s32[]{:T(128)}, f32[12,128,128]{2,1,0:T(8,128)S(1)}, f32[8,12,64,128]{3,2,0,1:T(8,128)}, f32[8,12,64,128]{3,2,0,1:T(8,128)}, f32[8,12,64]{2,0,1:T(8...) while((s32[]{:T(128)}, f32[12,128,128]{2,1,0:T(8,128)S(1)}, ...), condition=%wide.region_5.6_spmd, body=%wide.region_4.5_spmd.sunk | while | flops 831590464 | bytes 12349789 | solution.py:50
  416.7 59.0 %custom-call.8 = f32[12,1,64,64]{2,3,1,0:T(8,128)S(1)} custom-call(f32[12,1,64,64]{3,2,1,0:T(8,128)S(1)} %fusion.93), custom_call_target="InvertDiagBlocksLowerTriangular" | custom-call | tf_op jit(solution)/shard_map/while/body/eval_jaxpr/jit(_solve_triangular)/vmap()/triangular_solve | solution.py:28
  486.0 59.0 %custom-call.8 = f32[12,1,64,64]{2,3,1,0:T(8,128)S(1)} custom-call(f32[12,1,64,64]{3,2,1,0:T(8,128)S(1)} %fusion.93), custom_call_target="InvertDiagBlocksLowerTriangular" | custom-call | tf_op jit(solution)/shard_map/while/body/eval_jaxpr/jit(_solve_triangular)/vmap()/triangular_solve | solution.py:28
  555.4 59.0 %custom-call.8 = f32[12,1,64,64]{2,3,1,0:T(8,128)S(1)} custom-call(f32[12,1,64,64]{3,2,1,0:T(8,128)S(1)} %fusion.93), custom_call_target="InvertDiagBlocksLowerTriangular" | custom-call | tf_op jit(solution)/shard_map/while/body/eval_jaxpr/jit(_solve_triangular)/vmap()/triangular_solve | solution.py:28
  624.7 59.0 %custom-call.8 = f32[12,1,64,64]{2,3,1,0:T(8,128)S(1)} custom-call(f32[12,1,64,64]{3,2,1,0:T(8,128)S(1)} %fusion.93), custom_call_target="InvertDiagBlocksLowerTriangular" | custom-call | tf_op jit(solution)/shard_map/while/body/eval_jaxpr/jit(_solve_triangular)/vmap()/triangular_solve | solution.py:28
  694.0 59.0 %custom-call.8 = f32[12,1,64,64]{2,3,1,0:T(8,128)S(1)} custom-call(f32[12,1,64,64]{3,2,1,0:T(8,128)S(1)} %fusion.93), custom_call_target="InvertDiagBlocksLowerTriangular" | custom-call | tf_op jit(solution)/shard_map/while/body/eval_jaxpr/jit(_solve_triangular)/vmap()/triangular_solve | solution.py:28
  763.4 59.0 %custom-call.8 = f32[12,1,64,64]{2,3,1,0:T(8,128)S(1)} custom-call(f32[12,1,64,64]{3,2,1,0:T(8,128)S(1)} %fusion.93), custom_call_target="InvertDiagBlocksLowerTriangular" | custom-call | tf_op jit(solution)/shard_map/while/body/eval_jaxpr/jit(_solve_triangular)/vmap()/triangular_solve | solution.py:28
  832.7 59.0 %custom-call.8 = f32[12,1,64,64]{2,3,1,0:T(8,128)S(1)} custom-call(f32[12,1,64,64]{3,2,1,0:T(8,128)S(1)} %fusion.93), custom_call_target="InvertDiagBlocksLowerTriangular" | custom-call | tf_op jit(solution)/shard_map/while/body/eval_jaxpr/jit(_solve_triangular)/vmap()/triangular_solve | solution.py:28
  902.0 59.0 %custom-call.8 = f32[12,1,64,64]{2,3,1,0:T(8,128)S(1)} custom-call(f32[12,1,64,64]{3,2,1,0:T(8,128)S(1)} %fusion.93), custom_call_target="InvertDiagBlocksLowerTriangular" | custom-call | tf_op jit(solution)/shard_map/while/body/eval_jaxpr/jit(_solve_triangular)/vmap()/triangular_solve | solution.py:28
  978.6 8.2 convert_bitcast_fusion
  989.3 7.6 all-to-all-start.2
  997.2 5.3 copy.142
  1002.5 4.9 copy.143
  1007.4 9.9 multiply_convert_fusion.1
  1017.4 3.9 maximum_bitcast_fusion
  1021.3 5.7 reshape.308
  1030.9 4.2 broadcast_in_dim.32
  1035.1 8.4 scatter_fusion
  1043.5 8.4 all-to-all-start.3
  1053.5 139.6 %all-to-all-done.3 = bf16[32,128,2,512]{3,1,2,0:T(8,128)(2,1)} async-done(((bf16[32,128,2,512]{3,1,2,0:T(8,128)(2,1)}), bf16[32,128,2,512]{3,1,2,0:T(8,128)(2,1)}, u32[]{:S(2)}, u32[]{:S(2)}) %all-to-all-start.3) | async-done | bytes 8388640 | tf_op jit(solution)/shard_map/all_to_all | solution.py:185
  1195.2 17.1 %scatter_fusion.1 = bf16[12,128,2,512]{3,1,2,0:T(8,128)(2,1)} fusion(bf16[12,128,2,512]{3,1,2,0:T(8,128)(2,1)} %broadcast_in_dim.25, s32[32]{0:T(128)S(1)} %fusion.41, bf16[32,128,2,512]{3,1,2,0:T(8,128)(2,1)} %all-to-all-done.3), kind=kCustom, calls=%fused_computation.3 | custom fusion | bytes 25165952 | tf_op jit(solution)/shard_map/scatter | solution.py:189
  1212.3 6.8 copy.148
  (214 shorter events, 131.9 us)
Async XLA Ops:
  7.2 163.6 %copy-start = (bf16[1536,512]{1,0:T(8,128)(2,1)S(1)}, bf16[1536,512]{1,0:T(8,128)(2,1)}, u32[]{:S(2)}) copy-start(bf16[1536,512]{1,0:T(8,128)(2,1)} %param.13) | copy-start | bytes 4718596
  7.2 163.6 %all-gather.3.cloned.1.call-start = ((), (), s32[]{:S(2)}) async-start(), calls=%async_computation.6 | async-start | bytes 6488064 | tf_op jit(solution)/shard_map/all_gather | solution.py:93
  26.1 343.3 %reduce-scatter.3.cloned.1.call-start = ((), (), s32[]{:S(2)}) async-start(), calls=%async_computation.7 | async-start | bytes 23592960 | tf_op jit(solution)/shard_map/reduce_scatter | solution.py:98
  205.0 0.9 copy-start.3
  205.0 27.3 %copy-start.10 = (u32[128]{0:T(128)S(1)}, u32[128]{0:T(128)}, u32[]{:S(2)}) copy-start(u32[128]{0:T(128)} %constant.92) | copy-start | bytes 1540
  205.0 43.5 %copy-start.9 = (s32[3]{0:T(128)S(1)}, s32[3]{0:T(128)}, u32[]{:S(2)}) copy-start(s32[3]{0:T(128)} %param.22) | copy-start | bytes 40
  205.0 43.7 %copy-start.8 = (s32[3,4]{1,0:T(4,128)S(1)}, s32[3,4]{1,0:T(4,128)}, u32[]{:S(2)}) copy-start(s32[3,4]{1,0:T(4,128)} %param.21) | copy-start | bytes 148
  205.9 42.9 %copy-start.5 = (f32[4,1536]{1,0:T(4,128)S(1)}, f32[4,1536]{1,0:T(4,128)}, u32[]{:S(2)}) copy-start(f32[4,1536]{1,0:T(4,128)} %param.17) | copy-start | bytes 73732
  205.9 43.0 %copy-start.4 = (bf16[3,3,1536]{2,1,0:T(4,128)(2,1)S(1)}, bf16[3,3,1536]{2,1,0:T(4,128)(2,1)}, u32[]{:S(2)}) copy-start(bf16[3,3,1536]{2,1,0:T(4,128)(2,1)} %param.18) | copy-start | bytes 82948
  207.0 44.6 %all-to-all-start.1 = ((bf16[32,2,512]{2,1,0:T(2,128)(2,1)}), bf16[32,2,512]{2,1,0:T(2,128)(2,1)S(1)}, u32[]{:S(2)}, u32[]{:S(2)}) async-start(bf16[32,2,512]{2,1,0:T(2,128)(2,1)} %reshape.338), calls=%async_computation.1 | async-start | bytes 131072 | tf_op jit(solution)/shard_map/all_to_all | solution.py:87
  232.2 746.4 %all-gather.5.cloned.1.call-start = ((), (), s32[]{:S(2)}) async-start(), calls=%async_computation.8 | async-start | bytes 2162688 | tf_op jit(solution)/shard_map/all_gather | solution.py:94
  252.4 966.7 %reduce-scatter.5.cloned.1.call-start = ((), (), s32[]{:S(2)}) async-start(), calls=%async_computation.9 | async-start | bytes 7864320 | tf_op jit(solution)/shard_map/reduce_scatter | solution.py:150
  408.6 3.8 copy-start.2
  969.2 3.6 copy-start.7
  986.8 0.7 copy-start.6
  989.3 54.2 %all-to-all-start.2 = ((s32[32,1,1]{2,1,0:T(1,128)}), s32[32,1,1]{2,1,0:T(1,128)S(1)}, u32[]{:S(2)}, u32[]{:S(2)}) async-start(s32[32,1,1]{2,1,0:T(1,128)} %copy.140), calls=%async_computation.4 | async-start | bytes 32768 | tf_op jit(solution)/shard_map/all_to_all | solution.py:186
  1043.5 149.6 %all-to-all-start.3 = ((bf16[32,128,2,512]{3,1,2,0:T(8,128)(2,1)}), bf16[32,128,2,512]{3,1,2,0:T(8,128)(2,1)}, u32[]{:S(2)}, u32[]{:S(2)}) async-start(bf16[32,128,2,512]{3,1,2,0:T(8,128)(2,1)} %scatter_fusion), calls=%async_computation.5 | async-start | bytes 16777216 | tf_op jit(solution)/shard_map/all_to_all | solution.py:185
  1195.2 23.9 %copy-start.1 = (bf16[1536,512]{1,0:T(8,128)(2,1)S(1)}, bf16[1536,512]{1,0:T(8,128)(2,1)}, u32[]{:S(2)}) copy-start(bf16[1536,512]{1,0:T(8,128)(2,1)} %param.13) | copy-start | bytes 4718596
Sparse Core Ops, SparseCore 0:
  26.2 144.5 all-gather.2
  205.2 164.0 reduce-scatter.2
  371.7 135.9 all-gather.4
  987.0 64.7 reduce-scatter.4
where the time goes:
time: 1230 us
  other arithmetic  520 us (42%)
  waiting for transfers between devices  401 us (33%)
  local copies, waits for them, and re-layouts  121 us (10%)
  matrix products  96.3 us (8%)
  starting transfers between devices  41.4 us (3%)
  blocking collectives  30 us (2%)
  between operations  14.8 us (1%)
    another operation x32, other arithmetic, delta_block(): jax.scipy.linalg.solve_triangular(system, right_side, lower=True, unit_di...  473 us
    all_gather x1, waiting for transfers between devices, local(): lax.all_gather(server_in, 'col', axis=1, tiled=True)  145 us
    all_to_all x1, waiting for transfers between devices, local(): lax.all_to_all(outgoing, 'col', split_axis=0, concat_axis=0, tiled=True)  140 us
    reduce_scatter x1, waiting for transfers between devices, local(): lax.psum_scatter(product.reshape(local_tokens, lax.axis_size('row') * hea...  117 us
    all_to_all x1, starting transfers between devices, local(): lax.all_to_all(out_weight.astype(jnp.bfloat16), 'col', split_axis=1, conc...  25.2 us
  transfers between devices with their start and end apart: 7, of which 3 were waited for; matrix products, arithmetic and copies ran while one was open for 56% of the time, Pallas kernels for 0%

commit v1 on v0

v1 whole, which is shorter than its diff:
```python
import functools
import jax
import jax.numpy as jnp
from jax import lax
from jax.experimental import pallas as pl
from jax.experimental.pallas import tpu as pltpu
from jax.sharding import PartitionSpec as P

DK = 128
CONV = 4
SEQ = 512
PAGE = 128
PAGES_SEQ = 4
CHUNK = 128
ROWS = 4
XORS = (0, 2, 1, 3)
BF = jnp.bfloat16
F32 = jnp.float32


def mm(a, b, dims=((1,), (0,))):
    return lax.dot_general(a, b, (dims, ((), ())), preferred_element_type=F32)


def assemble(w_ref, scratch, cols):
    n_col = w_ref.shape[0]
    for c in range(n_col):
        for r in range(ROWS):
            scratch[r, c * 16 : (c + 1) * 16, :] = w_ref[c, r * 16 : (r + 1) * 16, :]


def proj_kernel(
    targets,
    lens,
    tok_ref,
    w_ref,
    beta_ref,
    taps_ref,
    prior_ref,
    q_ref,
    k_ref,
    v_ref,
    rate_ref,
    page_ref,
    w_scr,
    u_scr,
    kv_scr,
):
    prompt, pair, page = pl.program_id(1), pl.program_id(0), pl.program_id(2)
    width = u_scr.shape[1]

    @pl.when((prompt == 0) & (page == 0))
    def _():
        assemble(w_ref, w_scr, width)

    @pl.when(page == 0)
    def _():
        acc = mm(tok_ref[0], w_scr[0])
        for r in range(1, ROWS):
            acc += mm(tok_ref[r], w_scr[r])
        u_scr[8:, :] = acc
        u_scr[0:8, :] = prior_ref[0]

    @pl.when((page == 0) & (pair == 0))
    def _():
        logits = mm(tok_ref[0], beta_ref[0])
        for r in range(1, ROWS):
            logits += mm(tok_ref[r], beta_ref[r])
        rows = lax.broadcasted_iota(jnp.int32, (SEQ, DK), 0)
        live = rows < lens[prompt]
        rate_ref[...] = jnp.where(live, jax.nn.sigmoid(logits), 0.0)

    base = page * PAGE
    rows = base + lax.broadcasted_iota(jnp.int32, (PAGE, DK), 0)
    live = rows < lens[prompt]
    window = u_scr[pl.ds(pl.multiple_of(base, PAGE), PAGE + 8), :]
    heads = width // (3 * DK)
    for h in range(heads):
        for j in range(3):
            lo = (3 * h + j) * DK
            win = window[:, lo : lo + DK]
            total = taps_ref[0, lo : lo + DK][None, :] * win[5 : 5 + PAGE]
            for i in range(1, CONV):
                total += taps_ref[i, lo : lo + DK][None, :] * win[5 + i : 5 + i + PAGE]
            act = total * jax.nn.sigmoid(total)
            if j < 2:
                act = act * lax.rsqrt(jnp.sum(act * act, axis=1, keepdims=True) + 1e-06)
            if j == 0:
                q_ref[h] = act.astype(BF)
            else:
                act = jnp.where(live, act, 0.0)
                (k_ref, v_ref)[j - 1][h] = act.astype(BF)
                kv_scr[h, pl.ds(j - 1, PAGE, stride=2), :] = act
    for h in range(heads):
        page_ref[0, :, h * DK : (h + 1) * DK] = kv_scr[h].astype(BF)


def project(targets, lens, tok, w, beta, taps, prior, n_slots):
    prompts = lens.shape[0]
    n_cols = w.shape[2]
    heads = n_cols // (3 * DK)
    pair_n = 2
    pairs = heads // pair_n
    width = pair_n * 3 * DK
    grid_spec = pltpu.PrefetchScalarGridSpec(
        num_scalar_prefetch=2,
        grid=(pairs, prompts, PAGES_SEQ),
        in_specs=[
            pl.BlockSpec((ROWS, SEQ, tok.shape[2]), lambda a, p, g, t, n: (0, p, 0)),
            pl.BlockSpec((w.shape[0], w.shape[1], width), lambda a, p, g, t, n: (0, 0, a)),
            pl.BlockSpec(beta.shape, lambda a, p, g, t, n: (0, 0, 0)),
            pl.BlockSpec((CONV, width), lambda a, p, g, t, n: (0, a)),
            pl.BlockSpec((1, 8, width), lambda a, p, g, t, n: (p, 0, a)),
        ],
        out_specs=[
            pl.BlockSpec((pair_n, PAGE, DK), lambda a, p, g, t, n: (a, p * PAGES_SEQ + g, 0)),
            pl.BlockSpec((pair_n, PAGE, DK), lambda a, p, g, t, n: (a, p * PAGES_SEQ + g, 0)),
            pl.BlockSpec((pair_n, PAGE, DK), lambda a, p, g, t, n: (a, p * PAGES_SEQ + g, 0)),
            pl.BlockSpec((SEQ, DK), lambda a, p, g, t, n: (jnp.where(a == 0, p, prompts), 0)),
            pl.BlockSpec(
                (1, 2 * PAGE, pair_n * DK), lambda a, p, g, t, n: (t[p * PAGES_SEQ + g], 0, a)
            ),
        ],
        scratch_shapes=[
            pltpu.VMEM((ROWS, w.shape[0] * 16, width), BF),
            pltpu.VMEM((SEQ + 8, width), F32),
            pltpu.VMEM((pair_n, 2 * PAGE, DK), F32),
        ],
    )
    total = prompts * SEQ
    return pl.pallas_call(
        proj_kernel,
        grid_spec=grid_spec,
        out_shape=[
            jax.ShapeDtypeStruct((heads, total, DK), BF),
            jax.ShapeDtypeStruct((heads, total, DK), BF),
            jax.ShapeDtypeStruct((heads, total, DK), BF),
            jax.ShapeDtypeStruct((total + SEQ, DK), F32),
            jax.ShapeDtypeStruct((n_slots, 2 * PAGE, heads * DK), BF),
        ],
        compiler_params=pltpu.CompilerParams(vmem_limit_bytes=48 << 20),
        cost_estimate=pl.CostEstimate(
            flops=2 * total * 2048 * n_cols, bytes_accessed=24 << 20, transcendentals=total * n_cols
        ),
        name="project",
    )(targets, lens, tok, w, beta, taps, prior)


def scan_kernel(lens, index, q_ref, k_ref, v_ref, rate_ref, gain_ref, *rest):
    heads = q_ref.shape[0]
    starts, (out_ref, state_ref) = rest[:heads], rest[heads:]
    prompt = pl.program_id(0)
    n_chunk = SEQ // CHUNK
    ri = lax.broadcasted_iota(jnp.int32, (CHUNK, CHUNK), 0)
    ci = lax.broadcasted_iota(jnp.int32, (CHUNK, CHUNK), 1)
    diff = ri ^ ci
    lower = ri > ci
    eye = (ri == ci).astype(F32)
    causal = ri >= ci
    states = [starts[h][0, 0] for h in range(heads)]
    for c in range(n_chunk):
        rows = slice(c * CHUNK, (c + 1) * CHUNK)
        live = (c * CHUNK + ri) < lens[prompt]
        q = [q_ref[h, rows, :] for h in range(heads)]
        k = [k_ref[h, rows, :] for h in range(heads)]
        rate = [rate_ref[rows, h : h + 1] for h in range(heads)]
        gram = [mm(k[h], k[h], ((1,), (1,))) for h in range(heads)]
        strict = [jnp.where(lower, gram[h] * rate[h], 0.0) for h in range(heads)]
        inv = [eye - jnp.where(diff == 1, strict[h], 0.0) for h in range(heads)]
        level = 1
        while (2 << level) <= CHUNK:
            part = [
                jnp.where((diff >> level) == 1, strict[h], 0.0).astype(BF) for h in range(heads)
            ]
            low = [inv[h].astype(BF) for h in range(heads)]
            mid = [mm(part[h], low[h]).astype(BF) for h in range(heads)]
            inv = [inv[h] - mm(low[h], mid[h]) for h in range(heads)]
            level += 1
        scores = [
            jnp.where(causal, mm(q[h], k[h], ((1,), (1,))), 0.0).astype(BF) for h in range(heads)
        ]
        kf = [k[h].astype(F32) * rate[h] for h in range(heads)]
        vf = [v_ref[h, rows, :].astype(F32) * rate[h] for h in range(heads)]
        right = [jnp.concatenate([kf[h].astype(BF), vf[h].astype(BF)], axis=1) for h in range(heads)]
        solved = [mm(inv[h].astype(BF), right[h]) for h in range(heads)]
        for h in range(heads):
            sb = states[h].astype(BF)
            wq = jnp.concatenate([solved[h][:, :DK].astype(BF), q[h]], axis=0)
            both = mm(wq, sb)
            fixed = (solved[h][:, DK:] - both[:CHUNK]).astype(BF)
            out = both[CHUNK:] + mm(scores[h], fixed)
            states[h] = states[h] + mm(k[h], fixed, ((0,), (0,)))
            out = jnp.where(live, out, 0.0)
            scale = lax.rsqrt(jnp.mean(out * out, axis=1, keepdims=True) + 1e-05)
            gain = gain_ref[0:1, h * DK : (h + 1) * DK]
            out_ref[rows, h * DK : (h + 1) * DK] = (out * scale * gain).astype(BF)
    for h in range(heads):
        state_ref[0, h] = states[h]


def scan_all(lens, index, q, k, v, rate, gain, pool):
    heads = q.shape[0]
    prompts = lens.shape[0]
    qkv = pl.BlockSpec((heads, SEQ, DK), lambda p, n, i: (0, p, 0))

    def start_spec(h):
        return pl.BlockSpec((1, 1, DK, DK), lambda p, n, i: (i[p * heads + h], h, 0, 0))

    grid_spec = pltpu.PrefetchScalarGridSpec(
        num_scalar_prefetch=2,
        grid=(prompts,),
        in_specs=[
            qkv,
            qkv,
            qkv,
            pl.BlockSpec((SEQ, DK), lambda p, n, i: (p, 0)),
            pl.BlockSpec((1, heads * DK), lambda p, n, i: (0, 0)),
        ]
        + [start_spec(h) for h in range(heads)],
        out_specs=[
            pl.BlockSpec((SEQ, heads * DK), lambda p, n, i: (p, 0)),
            pl.BlockSpec((1, heads, DK, DK), lambda p, n, i: (p, 0, 0, 0)),
        ],
    )
    return pl.pallas_call(
        scan_kernel,
        grid_spec=grid_spec,
        out_shape=[
            jax.ShapeDtypeStruct((prompts * SEQ, heads * DK), BF),
            jax.ShapeDtypeStruct((prompts, heads, DK, DK), F32),
        ],
        compiler_params=pltpu.CompilerParams(vmem_limit_bytes=40 << 20),
        cost_estimate=pl.CostEstimate(
            flops=24 << 30, bytes_accessed=12 << 20, transcendentals=0
        ),
        name="delta",
    )(lens, index, q, k, v, rate, gain, *([pool] * heads))


def out_kernel(x_ref, w_ref, o_ref, w_scr):
    @pl.when(pl.program_id(0) == 0)
    def _():
        assemble(w_ref, w_scr, w_scr.shape[2])

    acc = mm(x_ref[0], w_scr[0])
    for r in range(1, ROWS):
        acc += mm(x_ref[r], w_scr[r])
    o_ref[...] = acc.astype(BF)


def out_product(x, w):
    total, n_cols = x.shape[1], w.shape[2]
    return pl.pallas_call(
        out_kernel,
        grid=(total // SEQ,),
        in_specs=[
            pl.BlockSpec((ROWS, SEQ, x.shape[2]), lambda p: (0, p, 0)),
            pl.BlockSpec(w.shape, lambda p: (0, 0, 0)),
        ],
        out_specs=pl.BlockSpec((SEQ, n_cols), lambda p: (p, 0)),
        out_shape=jax.ShapeDtypeStruct((total, n_cols), BF),
        scratch_shapes=[pltpu.VMEM((ROWS, w.shape[0] * 16, n_cols), BF)],
        compiler_params=pltpu.CompilerParams(vmem_limit_bytes=32 << 20),
        cost_estimate=pl.CostEstimate(
            flops=2 * total * 2048 * n_cols, bytes_accessed=10 << 20, transcendentals=0
        ),
        name="outmix",
    )(x, w)


def row_swap(x, k):
    return lax.ppermute(x, "row", [(r, r ^ k) for r in range(ROWS)])


def row_gather(x):
    near = row_swap(x, 2)
    mine = jnp.stack([x, near])
    return jnp.concatenate([mine, row_swap(mine, 1)], axis=0)


def col_gather(x):
    n_col = lax.axis_size("col")
    return lax.all_to_all(
        jnp.broadcast_to(x[None], (n_col,) + x.shape), "col", split_axis=0, concat_axis=0, tiled=True
    )


def local(
    tokens,
    in_weight,
    out_weight,
    beta_weight,
    conv_weight,
    conv_prior,
    head_gain,
    state_pool,
    state_index,
    lengths,
    page_table,
):
    n_col = lax.axis_size("col")
    row_id = lax.axis_index("row")
    span = tokens.shape[1]
    heads = state_index.shape[1]
    prompts = lengths.shape[0]
    n_pages = prompts * PAGES_SEQ
    part = in_weight.shape[0]
    in_cols = in_weight.shape[1] // ROWS
    out_cols = out_weight.shape[1] // ROWS

    win = in_weight.astype(BF)
    wout = out_weight.astype(BF)
    both = jnp.concatenate(
        [win.reshape(part, ROWS, in_cols), wout.reshape(part, ROWS, out_cols)], axis=2
    ).transpose(1, 0, 2)

    def piece(r):
        return lax.dynamic_index_in_dim(both, r, 0, keepdims=False)

    pieces = [piece(row_id)] + [row_swap(piece(row_id ^ k), k) for k in XORS[1:]]
    mine = jnp.concatenate(pieces, axis=0)
    wide_in = col_gather(mine[:, :in_cols])
    wide_out = col_gather(mine[:, in_cols:])

    tok_all = row_gather(tokens)

    targets = page_table[:, :, 0].reshape(-1)
    slots = page_table[:, :, 1].reshape(-1)
    hit = targets[:, None] == jnp.arange(n_col, dtype=jnp.int32)[None, :]
    slot_for = jnp.max(jnp.where(hit, slots[:, None], -1), axis=0)
    block_in, block_out = win.shape[1] // n_col, wout.shape[1] // n_col
    send = jnp.concatenate(
        [
            win.reshape(part, n_col, block_in).transpose(1, 0, 2).reshape(n_col, -1, DK),
            wout.reshape(part, n_col, block_out).transpose(1, 0, 2).reshape(n_col, -1, DK),
            jnp.broadcast_to(slot_for.astype(BF)[:, None, None], (n_col, 8, DK)),
        ],
        axis=1,
    )
    got = lax.all_to_all(send, "col", split_axis=0, concat_axis=0, tiled=True)
    n_in = part * block_in // DK
    n_out = part * block_out // DK
    server_in = got[:, :n_in].reshape(n_col * part, block_in)
    server_out = got[:, n_in : n_in + n_out].reshape(n_col * part, block_out)
    arrived_slots = got[:, n_in + n_out, 0].astype(jnp.int32)
    wanted = arrived_slots[None, :] == jnp.arange(n_pages, dtype=jnp.int32)[:, None]
    source = jnp.sum(
        jnp.where(wanted, jnp.arange(n_col, dtype=jnp.int32)[None, :], 0), axis=1
    ).astype(jnp.int32)

    beta = lax.dynamic_slice_in_dim(beta_weight, row_id * heads, heads, 1).astype(BF)
    beta = beta.reshape(ROWS, span, heads)
    beta = jnp.stack(
        [lax.dynamic_index_in_dim(beta, row_id ^ k, 0, keepdims=False) for k in XORS]
    )
    beta = jnp.pad(beta, ((0, 0), (0, 0), (0, DK - heads)))
    prior = jnp.pad(conv_prior.astype(F32), ((0, 0), (8 - (CONV - 1), 0), (0, 0)))

    q, k, v, rate, outgoing = project(
        targets, lengths, tok_all, wide_in, beta, conv_weight, prior, n_col
    )
    arrived = lax.all_to_all(outgoing, "col", split_axis=0, concat_axis=0, tiled=True)
    normed, final_state = scan_all(
        lengths, state_index.reshape(-1), q, k, v, rate, head_gain.reshape(1, -1), state_pool
    )
    layer_out = out_product(row_gather(normed), wide_out)
    page_cache = jnp.take(arrived, source, axis=0, mode="clip").reshape(
        n_pages, PAGE, 2, heads * DK
    )
    return (server_in, server_out, layer_out, final_state, page_cache)


def solution(mesh):
    return jax.shard_map(
        local,
        mesh=mesh,
        in_specs=(
            P("col", "row"),
            P(("row", "col"), None),
            P(("row", "col"), None),
            P(),
            P(None, "row"),
            P("col", None, "row"),
            P("row"),
            P("col", "row", None, None),
            P("col", "row"),
            P("col"),
            P("col", None, None),
        ),
        out_specs=(
            P("row", "col"),
            P("row", "col"),
            P("col", "row"),
            P("col", "row", None, None),
            P("col", None, None, "row"),
        ),
        check_vma=False,
    )
```

time: 1230 us -> 439 us (0.36)
  the two profiles are of different devices: /device:TPU:16 before, /device:TPU:43 now
where the time goes in v1:
time: 439 us; the launch traced here: 438 us
  waiting for transfers between devices  273 us (62%)
  Pallas kernels  76.2 us (17%)
  starting transfers between devices  39.4 us (9%)
  local copies, waits for them, and re-layouts  29.6 us (7%)
  other arithmetic  18 us (4%)
    ppermute x7, waiting for transfers between devices, row_swap(): return lax.ppermute(x, 'row', [(r, r ^ k) for r in range(ROWS)])  273 us
    pallas_call x1, Pallas kernels, project(): pl.pallas_call(proj_kernel, grid_spec=grid_spec, out_shape=[jax.ShapeDtyp...  36.2 us
    pallas_call x1, Pallas kernels, scan_all(): pl.pallas_call(scan_kernel, grid_spec=grid_spec, out_shape=[jax.ShapeDtyp...  34.9 us
    unnamed x43, local copies, waits for them, and re-layouts  12.8 us
    all_to_all x2, starting transfers between devices, col_gather(): lax.all_to_all(jnp.broadcast_to(x[None], (n_col,) + x.shape), 'col', spli...  12.7 us
    ppermute x7, starting transfers between devices, row_swap(): return lax.ppermute(x, 'row', [(r, r ^ k) for r in range(ROWS)])  10.4 us
    concatenate x2, other arithmetic, row_gather(): return jnp.concatenate([mine, row_swap(mine, 1)], axis=0)  9.47 us
  transfers between devices with their start and end apart: 11, of which 5 were waited for; matrix products, arithmetic and copies ran while one was open for 5% of the time, Pallas kernels for 17%

profile of v1, /device:TPU:43, one launch (start us, length us, event | category | flops | bytes accessed | tf_op | source)
XLA Modules:
  0.0 437.6 jit_solution(9700399633910804142)
XLA Ops:
  5.7 8.4 %all-to-all-start = ((bf16[32,40,128]{2,1,0:T(8,128)(2,1)}), bf16[32,40,128]{2,1,0:T(8,128)(2,1)S(1)}, u32[]{:S(2)}, u32[]{:S(2)}) async-start(bf16[32,40,128]{2,1,0:T(8,128)(2,1)} %pad_maximum_fusion.4), calls=%async_computation | async-start | bytes 655360 | tf_op jit(solution)/shard_map/all_to_all | solution.py:340
  15.1 1.9 collective-permute-start.2
  17.1 1.6 collective-permute-start.3
  20.8 3.2 collective-permute-done.4
  24.8 3.3 broadcast_in_dim.54
  28.1 7.9 %all-to-all-start.1 = ((bf16[32,64,1536]{2,1,0:T(8,128)(2,1)}), bf16[32,64,1536]{2,1,0:T(8,128)(2,1)}, u32[]{:S(2)}, u32[]{:S(2)}) async-start(bf16[32,64,1536]{2,1,0:T(8,128)(2,1)} %broadcast_in_dim.54), calls=%async_computation.1 | async-start | bytes 12582912 | tf_op jit(solution)/shard_map/all_to_all | solution.py:283
  36.0 1.2 collective-permute-start
  37.2 135.9 %collective-permute-done = bf16[1536,512]{1,0:T(8,128)(2,1)S(1)} collective-permute-done((bf16[1536,512]{1,0:T(8,128)(2,1)S(1)}, bf16[1536,512]{1,0:T(8,128)(2,1)S(1)}, u32[]{:S(2)}, u32[]{:S(2)}) %collective-permute-start) | collective-permute-done | bytes 1572896 | tf_op jit(solution)/shard_map/ppermute | solution.py:272
  173.2 2.1 pad_maximum_fusion.2
  175.4 1.2 collective-permute-start.1
  176.5 1.5 broadcast_in_dim.55
  178.1 4.8 %all-to-all-start.2 = ((bf16[32,64,512]{2,1,0:T(8,128)(2,1)}), bf16[32,64,512]{2,1,0:T(8,128)(2,1)S(1)}, u32[]{:S(2)}, u32[]{:S(2)}) async-start(bf16[32,64,512]{2,1,0:T(8,128)(2,1)} %broadcast_in_dim.55), calls=%async_computation.2 | async-start | bytes 4194304 | tf_op jit(solution)/shard_map/all_to_all | solution.py:283
  183.7 6.4 %pad_maximum_fusion.tok_ref = bf16[4,1536,512]{2,1,0:T(8,128)(2,1)} fusion(bf16[2,1536,512]{2,1,0:T(8,128)(2,1)} %collective-permute-done.1, bf16[1,1536,512]{2,1,0:T(8,128)(2,1)} %bitcast.30, bf16[1,1536,512]{2,1,0:T(8,128)(2,1)} %bitcast.27), kind=kLoop, calls=%fused_computation.1 | loop fusion | flops 6291456 | bytes 12582912 | tf_op jit(solution)/shard_map/concatenate | solution.py:278
  190.1 36.2 %project.1 = (bf16[4,1536,128]{2,1,0:T(8,128)(2,1)S(1)}, bf16[4,1536,128]{2,1,0:T(8,128)(2,1)S(1)}, bf16[4,1536,128]{2,1,0:T(8,128)(2,1)}, f32[2048,128]{1,0:T(8,128)S(1)}, bf16[32,256,512]{2,1,0:T(8,128)(2,1)}) custom-call(s32[12]{0:T(128)S(1)} %eq.30.targets, s32[3]{0:T(128)S(1)} %copy-done.7, bf16[4,1536,512]{2,1,0:T(8,128)(2,1)} %pad_maximum_fusion.tok_ref, ...), custom_call_target="tpu_custom_call" | custom-call | flops 9663676416 | bytes 25165824 | tf_op jit(solution)/shard_map/project/pallas_call | solution.py:131
  227.4 1.2 copy-done.10
  228.6 1.3 copy-done.2
  229.9 7.8 %all-to-all-start.3 = ((bf16[32,256,512]{2,1,0:T(8,128)(2,1)}), bf16[32,256,512]{2,1,0:T(8,128)(2,1)}, u32[]{:S(2)}, u32[]{:S(2)}) async-start(bf16[32,256,512]{2,1,0:T(8,128)(2,1)} %get-tuple-element.18), calls=%async_computation.3 | async-start | bytes 16777216 | tf_op jit(solution)/shard_map/all_to_all | solution.py:362
  237.8 1.4 copy-done.4
  239.2 1.4 copy-done.9
  240.6 1.4 copy-done.11
  242.0 1.4 copy-done.12
  243.4 34.9 %delta.1 = (bf16[1536,512]{1,0:T(8,128)(2,1)S(1)}, f32[3,4,128,128]{3,2,1,0:T(8,128)}) custom-call(s32[3]{0:T(128)S(1)} %copy-done.7, s32[12]{0:T(128)S(1)} %reshape.74.index, bf16[4,1536,128]{2,1,0:T(8,128)(2,1)S(1)} %copy-done.9, bf16[4,1536,128]{2,1,0:T(8,128)(2,1)S(1)} %copy-done.11, bf16[4,1536,128]{2,1,0:T(8,128)(2,1)S(1)} %copy-done.12, ...), custom_call_target="tpu_custom_call" | custom-call | flops 25769803776 | bytes 12582912 | tf_op jit(solution)/shard_map/delta/pallas_call | solution.py:225
  278.3 1.8 collective-permute-start.5
  280.1 132.7 %collective-permute-done.5 = bf16[1536,512]{1,0:T(8,128)(2,1)S(1)} collective-permute-done((bf16[1536,512]{1,0:T(8,128)(2,1)S(1)}, bf16[1536,512]{1,0:T(8,128)(2,1)S(1)}, u32[]{:S(2)}, u32[]{:S(2)}) %collective-permute-start.5) | collective-permute-done | bytes 1572896 | tf_op jit(solution)/shard_map/ppermute | solution.py:272
  412.9 1.9 pad_maximum_fusion.3
  414.8 1.6 collective-permute-start.6
  417.2 1.8 copy.46
  419.8 1.5 fusion
  422.0 3.0 pad_maximum_fusion.1.x_ref
  425.0 5.1 %outmix.1 = bf16[1536,512]{1,0:T(8,128)(2,1)} custom-call(bf16[4,1536,512]{2,1,0:T(8,128)(2,1)S(1)} %pad_maximum_fusion.1.x_ref, bf16[32,64,512]{2,1,0:T(8,128)(2,1)S(1)} %copy-done.3), custom_call_target="tpu_custom_call" | custom-call | flops 3221225472 | bytes 10485760 | tf_op jit(solution)/shard_map/outmix/pallas_call | solution.py:253
  430.2 4.2 gather_fusion
  434.4 3.2 reshape.79
  (82 shorter events, 13.1 us)
Async XLA Ops:
  0.6 182.3 %copy-start = (f32[2048,16]{0,1:T(8,128)S(1)}, f32[2048,16]{0,1:T(8,128)}, u32[]{:S(2)}) copy-start(f32[2048,16]{0,1:T(8,128)} %param.14) | copy-start | bytes 393220
  5.7 18.4 %all-to-all-start = ((bf16[32,40,128]{2,1,0:T(8,128)(2,1)}), bf16[32,40,128]{2,1,0:T(8,128)(2,1)S(1)}, u32[]{:S(2)}, u32[]{:S(2)}) async-start(bf16[32,40,128]{2,1,0:T(8,128)(2,1)} %pad_maximum_fusion.4), calls=%async_computation | async-start | bytes 655360 | tf_op jit(solution)/shard_map/all_to_all | solution.py:340
  15.1 5.7 %collective-permute-start.2 = (bf16[16,2048]{1,0:T(8,128)(2,1)S(1)}, bf16[16,2048]{1,0:T(8,128)(2,1)S(1)}, u32[]{:S(2)}, u32[]{:S(2)}) collective-permute-start(bf16[16,2048]{1,0:T(8,128)(2,1)S(1)} %bitcast.37), channel_id=1, source_target_pairs={{0,64},{32,96},{64,0},{96,32},{1,65},{33,97},{65,1},{97,33},{2,66}... | collective-permute-start | bytes 196616 | tf_op jit(solution)/shard_map/ppermute | solution.py:272
  17.1 3.7 collective-permute-start.3
  18.7 5.3 %collective-permute-start.4 = (bf16[16,2048]{1,0:T(8,128)(2,1)S(1)}, bf16[16,2048]{1,0:T(8,128)(2,1)S(1)}, u32[]{:S(2)}, u32[]{:S(2)}) collective-permute-start(bf16[16,2048]{1,0:T(8,128)(2,1)S(1)} %bitcast.39), channel_id=1, source_target_pairs={{0,96},{32,64},{64,32},{96,0},{1,97},{33,65},{65,33},{97,1},{2,98}... | collective-permute-start | bytes 196616 | tf_op jit(solution)/shard_map/ppermute | solution.py:272
  24.1 0.7 copy-start.15
  28.1 7.9 %copy-start.13 = (bf16[1536,512]{1,0:T(8,128)(2,1)S(1)}, bf16[1536,512]{1,0:T(8,128)(2,1)}, u32[]{:S(2)}) copy-start(bf16[1536,512]{1,0:T(8,128)(2,1)} %param.11) | copy-start | bytes 4718596
  28.1 148.4 %all-to-all-start.1 = ((bf16[32,64,1536]{2,1,0:T(8,128)(2,1)}), bf16[32,64,1536]{2,1,0:T(8,128)(2,1)}, u32[]{:S(2)}, u32[]{:S(2)}) async-start(bf16[32,64,1536]{2,1,0:T(8,128)(2,1)} %broadcast_in_dim.54), calls=%async_computation.1 | async-start | bytes 12582912 | tf_op jit(solution)/shard_map/all_to_all | solution.py:283
  36.0 137.1 %collective-permute-start = (bf16[1536,512]{1,0:T(8,128)(2,1)S(1)}, bf16[1536,512]{1,0:T(8,128)(2,1)S(1)}, u32[]{:S(2)}, u32[]{:S(2)}) collective-permute-start(bf16[1536,512]{1,0:T(8,128)(2,1)S(1)} %copy-done.13), channel_id=1, source_target_pairs={{0,64},{32,96},{64,0},{96,32},{1,65},{33,97},{65,1},{97,33},{2,66}... | collective-permute-start | bytes 4718600 | tf_op jit(solution)/shard_map/ppermute | solution.py:272
  173.2 2.2 copy-start.14
  175.4 8.3 %collective-permute-start.1 = (bf16[2,1536,512]{2,1,0:T(8,128)(2,1)}, bf16[2,1536,512]{2,1,0:T(8,128)(2,1)}, u32[]{:S(2)}, u32[]{:S(2)}) collective-permute-start(bf16[2,1536,512]{2,1,0:T(8,128)(2,1)} %pad_maximum_fusion.2), channel_id=1, source_target_pairs={{0,32},{32,0},{64,96},{96,64},{1,33},{33,1},{65,97},{97,65},{2,34}... | collective-permute-start | bytes 9437192 | tf_op jit(solution)/shard_map/ppermute | solution.py:272
  176.5 6.8 %copy-start.17 = (s32[3,4]{1,0:T(4,128)S(1)}, s32[3,4]{1,0:T(4,128)}, u32[]{:S(2)}) copy-start(s32[3,4]{1,0:T(4,128)} %param.19) | copy-start | bytes 148
  178.1 5.5 %copy-start.16 = (bf16[3,3,1536]{2,1,0:T(4,128)(2,1)S(1)}, bf16[3,3,1536]{2,1,0:T(4,128)(2,1)}, u32[]{:S(2)}) copy-start(bf16[3,3,1536]{2,1,0:T(4,128)(2,1)} %param.16) | copy-start | bytes 82948
  178.1 50.5 %all-to-all-start.2 = ((bf16[32,64,512]{2,1,0:T(8,128)(2,1)}), bf16[32,64,512]{2,1,0:T(8,128)(2,1)S(1)}, u32[]{:S(2)}, u32[]{:S(2)}) async-start(bf16[32,64,512]{2,1,0:T(8,128)(2,1)} %broadcast_in_dim.55), calls=%async_computation.2 | async-start | bytes 4194304 | tf_op jit(solution)/shard_map/all_to_all | solution.py:283
  183.6 6.5 %copy-start.5 = (f32[4,1536]{1,0:T(4,128)S(1)}, f32[4,1536]{1,0:T(4,128)}, u32[]{:S(2)}) copy-start(f32[4,1536]{1,0:T(4,128)} %taps_ref.1) | copy-start | bytes 73732
  183.6 6.5 %copy-start.7 = (s32[3]{0:T(128)S(1)}, s32[3]{0:T(128)}, u32[]{:S(2)}) copy-start(s32[3]{0:T(128)} %lens.3) | copy-start | bytes 40
  226.3 1.1 copy-start.8
  227.4 1.2 copy-start.10
  228.6 1.3 copy-start.2
  228.6 9.2 %copy-start.6 = (f32[512]{0:T(512)S(1)}, f32[512]{0:T(512)}, u32[]{:S(2)}) copy-start(f32[512]{0:T(512)} %param.17) | copy-start | bytes 6148
  229.9 200.3 %all-to-all-start.3 = ((bf16[32,256,512]{2,1,0:T(8,128)(2,1)}), bf16[32,256,512]{2,1,0:T(8,128)(2,1)}, u32[]{:S(2)}, u32[]{:S(2)}) async-start(bf16[32,256,512]{2,1,0:T(8,128)(2,1)} %get-tuple-element.18), calls=%async_computation.3 | async-start | bytes 16777216 | tf_op jit(solution)/shard_map/all_to_all | solution.py:362
  237.8 1.4 copy-start.4
  239.2 1.4 copy-start.9
  240.6 1.4 copy-start.11
  242.0 1.4 copy-start.12
  278.3 134.6 %collective-permute-start.5 = (bf16[1536,512]{1,0:T(8,128)(2,1)S(1)}, bf16[1536,512]{1,0:T(8,128)(2,1)S(1)}, u32[]{:S(2)}, u32[]{:S(2)}) collective-permute-start(bf16[1536,512]{1,0:T(8,128)(2,1)S(1)} %get-tuple-element.16), channel_id=1, source_target_pairs={{0,64},{32,96},{64,0},{96,32},{1,65},{33,97},{65,1},{97,33},{2,66}... | collective-permute-start | bytes 4718600 | tf_op jit(solution)/shard_map/ppermute | solution.py:272
  412.9 3.5 slice-start
  412.9 6.1 %slice-start.1 = ((bf16[32,40,128]{2,1,0:T(8,128)(2,1)}), bf16[32,8,128]{2,1,0:T(8,128)(2,1)S(1)}, s32[]{:S(2)}) async-start(bf16[32,40,128]{2,1,0:T(8,128)(2,1)} %copy-done.15), calls=%async_computation.5 | async-start | bytes 131072 | tf_op jit(solution)/shard_map/slice | solution.py:344
  414.8 7.2 %collective-permute-start.6 = (bf16[2,1536,512]{2,1,0:T(8,128)(2,1)}, bf16[2,1536,512]{2,1,0:T(8,128)(2,1)}, u32[]{:S(2)}, u32[]{:S(2)}) collective-permute-start(bf16[2,1536,512]{2,1,0:T(8,128)(2,1)} %pad_maximum_fusion.3), channel_id=1, source_target_pairs={{0,32},{32,0},{64,96},{96,64},{1,33},{33,1},{65,97},{97,65},{2,34}... | collective-permute-start | bytes 9437192 | tf_op jit(solution)/shard_map/ppermute | solution.py:272
  421.5 3.6 copy-start.3
  430.2 7.4 %copy-start.1 = (f32[2048,16]{0,1:T(8,128)S(1)}, f32[2048,16]{0,1:T(8,128)}, u32[]{:S(2)}) copy-start(f32[2048,16]{0,1:T(8,128)} %param.14) | copy-start | bytes 393220

commit v2 on v1

v2 whole, which is shorter than its diff:
```python
import functools
import jax
import jax.numpy as jnp
from jax import lax
from jax.experimental import pallas as pl
from jax.experimental.pallas import tpu as pltpu
from jax.sharding import PartitionSpec as P

DK = 128
CONV = 4
SEQ = 512
PAGE = 128
PAGES_SEQ = 4
CHUNK = 128
ROWS = 4
XORS = (0, 2, 1, 3)
BF = jnp.bfloat16
F32 = jnp.float32


def mm(a, b, dims=((1,), (0,))):
    return lax.dot_general(a, b, (dims, ((), ())), preferred_element_type=F32)


def assemble(spots, pieces, scratch, col=None):
    j = 0
    width = pieces[0].shape[2]
    for ref in pieces:
        for i in range(ref.shape[0]):
            at = pl.ds(pl.multiple_of(spots[j] * 16, 16), 16)
            for r in range(ROWS):
                block = ref[i, r * 16 : (r + 1) * 16, :]
                if col is None:
                    scratch[r, at, :] = block
                else:
                    scratch[r, at, col : col + width] = block
            j += 1


def proj_kernel(with_rate, n_piece, n_after, targets, lens, spots, *refs):
    toks, refs = refs[:ROWS], refs[ROWS:]
    pieces, refs = refs[:n_piece], refs[n_piece:]
    if with_rate:
        beta_ref, refs = refs[0], refs[1:]
    refs = refs[:2] + refs[2 + n_after :]
    taps_ref, prior_ref, q_ref, k_ref, v_ref, page_ref = refs[:6]
    if with_rate:
        rate_ref = refs[6]
    w_scr, u_scr, kv_scr = refs[-3:]
    prompt, page = pl.program_id(0), pl.program_id(1)
    width = u_scr.shape[1]

    @pl.when((prompt == 0) & (page == 0))
    def _():
        assemble(spots, pieces, w_scr)

    @pl.when(page == 0)
    def _():
        acc = mm(toks[0][...], w_scr[0])
        for r in range(1, ROWS):
            acc += mm(toks[r][...], w_scr[r])
        u_scr[8:, :] = acc
        u_scr[0:8, :] = prior_ref[0]
        if with_rate:
            logits = mm(toks[0][...], beta_ref[0])
            for r in range(1, ROWS):
                logits += mm(toks[r][...], beta_ref[r])
            spot = lax.broadcasted_iota(jnp.int32, (SEQ, DK), 0)
            rate_ref[...] = jnp.where(spot < lens[prompt], jax.nn.sigmoid(logits), 0.0)

    base = page * PAGE
    live = base + lax.broadcasted_iota(jnp.int32, (PAGE, DK), 0) < lens[prompt]
    window = u_scr[pl.ds(pl.multiple_of(base, PAGE), PAGE + 8), :]
    heads = width // (3 * DK)
    for h in range(heads):
        for j in range(3):
            lo = (3 * h + j) * DK
            win = window[:, lo : lo + DK]
            total = taps_ref[0, lo : lo + DK][None, :] * win[5 : 5 + PAGE]
            for i in range(1, CONV):
                total += taps_ref[i, lo : lo + DK][None, :] * win[5 + i : 5 + i + PAGE]
            act = total * jax.nn.sigmoid(total)
            if j < 2:
                act = act * lax.rsqrt(jnp.sum(act * act, axis=1, keepdims=True) + 1e-06)
            if j == 0:
                q_ref[h] = act.astype(BF)
            else:
                act = jnp.where(live, act, 0.0)
                (k_ref, v_ref)[j - 1][h] = act.astype(BF)
                kv_scr[h, pl.ds(j - 1, PAGE, stride=2), :] = act
    for h in range(heads):
        page_ref[0, :, h * DK : (h + 1) * DK] = kv_scr[h].astype(BF)


def project(pair, targets, lens, spots, toks, pieces, beta, taps, prior, n_slots, after=()):
    prompts = lens.shape[0]
    pair_n = 2
    width = pair_n * 3 * DK
    with_rate = beta is not None
    total = prompts * SEQ
    span = toks[0].shape[1]

    def whole(x):
        return pl.BlockSpec((x.shape[0], x.shape[1], width), lambda p, g, t, n, c: (0, 0, 0))

    in_specs = [pl.BlockSpec((SEQ, span), lambda p, g, t, n, c: (p, 0))] * ROWS
    in_specs += [whole(x) for x in pieces]
    operands = [*toks, *pieces]
    if with_rate:
        in_specs += [pl.BlockSpec(beta.shape, lambda p, g, t, n, c: (0, 0, 0))]
        operands += [beta]
    in_specs += [
        pl.BlockSpec((CONV, width), lambda p, g, t, n, c: (0, pair)),
        pl.BlockSpec((1, 8, width), lambda p, g, t, n, c: (p, 0, pair)),
    ]
    in_specs += [pl.BlockSpec(memory_space=pl.ANY)] * len(after)
    operands += [taps, prior, *after]
    head_spec = pl.BlockSpec((pair_n, PAGE, DK), lambda p, g, t, n, c: (0, p * PAGES_SEQ + g, 0))
    out_specs = [head_spec] * 3 + [
        pl.BlockSpec((1, 2 * PAGE, pair_n * DK), lambda p, g, t, n, c: (t[p * PAGES_SEQ + g], 0, 0))
    ]
    out_shape = [jax.ShapeDtypeStruct((pair_n, total, DK), BF)] * 3 + [
        jax.ShapeDtypeStruct((n_slots, 2 * PAGE, pair_n * DK), BF)
    ]
    if with_rate:
        out_specs += [pl.BlockSpec((SEQ, DK), lambda p, g, t, n, c: (p, 0))]
        out_shape += [jax.ShapeDtypeStruct((total, DK), F32)]
    grid_spec = pltpu.PrefetchScalarGridSpec(
        num_scalar_prefetch=3,
        grid=(prompts, PAGES_SEQ),
        in_specs=in_specs,
        out_specs=out_specs,
        scratch_shapes=[
            pltpu.VMEM((ROWS, spots.shape[0] * 16, width), BF),
            pltpu.VMEM((SEQ + 8, width), F32),
            pltpu.VMEM((pair_n, 2 * PAGE, DK), F32),
        ],
    )
    return pl.pallas_call(
        functools.partial(proj_kernel, with_rate, len(pieces), len(after)),
        grid_spec=grid_spec,
        out_shape=out_shape,
        compiler_params=pltpu.CompilerParams(vmem_limit_bytes=56 << 20),
        cost_estimate=pl.CostEstimate(
            flops=2 * total * 2048 * width, bytes_accessed=14 << 20, transcendentals=total * width
        ),
        name="project",
    )(targets, lens, spots, *operands)


def scan_kernel(pair, lens, index, q_ref, k_ref, v_ref, rate_ref, gain_ref, pool_ref, *rest):
    heads = q_ref.shape[0]
    prompts = q_ref.shape[1] // SEQ
    n_heads = pool_ref.shape[1]
    first = pair * heads
    out_ref, state_ref, state_scr = rest[-3:]
    ri = lax.broadcasted_iota(jnp.int32, (CHUNK, CHUNK), 0)
    ci = lax.broadcasted_iota(jnp.int32, (CHUNK, CHUNK), 1)
    diff = ri ^ ci
    lower = ri > ci
    eye = (ri == ci).astype(F32)
    causal = ri >= ci
    seqs = [(p, h) for p in range(prompts) for h in range(heads)]
    every = range(len(seqs))
    for n, (p, h) in enumerate(seqs):
        state_scr[n] = pool_ref[index[p * n_heads + first + h], first + h]

    @pl.loop(0, SEQ // CHUNK)
    def _(c):
        at = [pl.ds(pl.multiple_of(p * SEQ + c * CHUNK, CHUNK), CHUNK) for p in range(prompts)]
        q = [q_ref[h, at[p], :] for p, h in seqs]
        k = [k_ref[h, at[p], :] for p, h in seqs]
        v = [v_ref[h, at[p], :] for p, h in seqs]
        rate = [rate_ref[at[p], first + h : first + h + 1] for p, h in seqs]
        gram = [mm(k[n], k[n], ((1,), (1,))) for n in every]
        strict = [jnp.where(lower, gram[n] * rate[n], 0.0) for n in every]
        inv = [eye - jnp.where(diff == 1, strict[n], 0.0) for n in every]
        level = 1
        while (2 << level) <= CHUNK:
            part = [jnp.where((diff >> level) == 1, strict[n], 0.0).astype(BF) for n in every]
            low = [inv[n].astype(BF) for n in every]
            mid = [mm(part[n], low[n]).astype(BF) for n in every]
            inv = [inv[n] - mm(low[n], mid[n]) for n in every]
            level += 1
        scores = [
            jnp.where(causal, mm(q[n], k[n], ((1,), (1,))), 0.0).astype(BF) for n in every
        ]
        right = [
            jnp.concatenate(
                [(k[n].astype(F32) * rate[n]).astype(BF), (v[n].astype(F32) * rate[n]).astype(BF)],
                axis=1,
            )
            for n in every
        ]
        solved = [mm(inv[n].astype(BF), right[n]) for n in every]
        state = [state_scr[n] for n in every]
        both = [
            mm(
                jnp.concatenate([solved[n][:, :DK].astype(BF), q[n]], axis=0),
                state[n].astype(BF),
            )
            for n in every
        ]
        fixed = [(solved[n][:, DK:] - both[n][:CHUNK]).astype(BF) for n in every]
        for n in every:
            state_scr[n] = state[n] + mm(k[n], fixed[n], ((0,), (0,)))
        for n, (p, h) in enumerate(seqs):
            out = both[n][CHUNK:] + mm(scores[n], fixed[n])
            out = jnp.where(c * CHUNK + ri < lens[p], out, 0.0)
            scale = lax.rsqrt(jnp.mean(out * out, axis=1, keepdims=True) + 1e-05)
            gain = gain_ref[0:1, h * DK : (h + 1) * DK]
            out_ref[at[p], h * DK : (h + 1) * DK] = (out * scale * gain).astype(BF)

    for n, (p, h) in enumerate(seqs):
        state_ref[p, h] = state_scr[n]


def scan_pair(pair, lens, index, q, k, v, rate, gain, pool, state=None):
    heads = q.shape[0]
    prompts = lens.shape[0]
    n_heads = pool.shape[1]
    total = prompts * SEQ
    qkv = pl.BlockSpec((heads, total, DK), lambda p, n, i: (0, 0, 0))
    in_specs = [qkv] * 3 + [
        pl.BlockSpec((total, DK), lambda p, n, i: (0, 0)),
        pl.BlockSpec((1, heads * DK), lambda p, n, i: (0, pair)),
        pl.BlockSpec(pool.shape, lambda p, n, i: (0, 0, 0, 0)),
    ]
    operands = [lens, index, q, k, v, rate, gain, pool]
    aliases = {}
    if state is not None:
        aliases = {len(operands): 1}
        in_specs += [pl.BlockSpec(memory_space=pl.ANY)]
        operands += [state]
    grid_spec = pltpu.PrefetchScalarGridSpec(
        num_scalar_prefetch=2,
        grid=(1,),
        in_specs=in_specs,
        out_specs=[
            pl.BlockSpec((total, heads * DK), lambda p, n, i: (0, 0)),
            pl.BlockSpec((prompts, heads, DK, DK), lambda p, n, i: (0, pair, 0, 0)),
        ],
        scratch_shapes=[pltpu.VMEM((prompts * heads, DK, DK), F32)],
    )
    return pl.pallas_call(
        functools.partial(scan_kernel, pair),
        grid_spec=grid_spec,
        out_shape=[
            jax.ShapeDtypeStruct((prompts * SEQ, heads * DK), BF),
            jax.ShapeDtypeStruct((prompts, n_heads, DK, DK), F32),
        ],
        input_output_aliases=aliases,
        compiler_params=pltpu.CompilerParams(vmem_limit_bytes=56 << 20),
        cost_estimate=pl.CostEstimate(flops=12 << 30, bytes_accessed=6 << 20, transcendentals=0),
        name="delta",
    )(*operands)


def out_kernel(n_piece, spots, *refs):
    xs, refs = refs[: 2 * ROWS], refs[2 * ROWS :]
    halves = (refs[:n_piece], refs[n_piece : 2 * n_piece])
    o_ref, w_scr = refs[2 * n_piece :]
    width = w_scr.shape[2] // 2

    @pl.when(pl.program_id(0) == 0)
    def _():
        for s in range(2):
            assemble(spots.at[s], halves[s], w_scr, s * width)

    span = xs[0].shape[1]
    acc = 0.0
    for j in range(2):
        for r in range(ROWS):
            acc += mm(xs[j * ROWS + r][...], w_scr[r, j * span : (j + 1) * span, :])
    o_ref[...] = acc.astype(BF)


def out_product(spots, xs, halves, in_cols, out_cols):
    total, span = xs[0].shape

    def tail(x):
        return pl.BlockSpec(
            (x.shape[0], x.shape[1], out_cols), lambda p, c: (0, 0, in_cols // out_cols)
        )

    grid_spec = pltpu.PrefetchScalarGridSpec(
        num_scalar_prefetch=1,
        grid=(total // SEQ,),
        in_specs=[pl.BlockSpec((SEQ, span), lambda p, c: (p, 0))] * (2 * ROWS)
        + [tail(x) for half in halves for x in half],
        out_specs=pl.BlockSpec((SEQ, 2 * out_cols), lambda p, c: (p, 0)),
        scratch_shapes=[pltpu.VMEM((ROWS, spots.shape[1] * 16, 2 * out_cols), BF)],
    )
    return pl.pallas_call(
        functools.partial(out_kernel, len(halves[0])),
        grid_spec=grid_spec,
        out_shape=jax.ShapeDtypeStruct((total, 2 * out_cols), BF),
        compiler_params=pltpu.CompilerParams(vmem_limit_bytes=32 << 20),
        cost_estimate=pl.CostEstimate(
            flops=4 * total * 2048 * out_cols, bytes_accessed=10 << 20, transcendentals=0
        ),
        name="outmix",
    )(spots, *xs, *halves[0], *halves[1])


def place_kernel(source, x0, x1, after, o_ref):
    width = x0.shape[2]
    for j, ref in enumerate((x0, x1)):
        o_ref[0, :, :, j * width : (j + 1) * width] = ref[0].reshape(PAGE, 2, width)


def place_pages(source, came0, came1, n_pages, after):
    width = came0.shape[2]
    spec = pl.BlockSpec((1, 2 * PAGE, width), lambda i, s: (s[i], 0, 0))
    grid_spec = pltpu.PrefetchScalarGridSpec(
        num_scalar_prefetch=1,
        grid=(n_pages,),
        in_specs=[spec, spec, pl.BlockSpec(memory_space=pl.ANY)],
        out_specs=pl.BlockSpec((1, PAGE, 2, 2 * width), lambda i, s: (i, 0, 0, 0)),
    )
    return pl.pallas_call(
        place_kernel,
        grid_spec=grid_spec,
        out_shape=jax.ShapeDtypeStruct((n_pages, PAGE, 2, 2 * width), BF),
        cost_estimate=pl.CostEstimate(flops=0, bytes_accessed=6 << 20, transcendentals=0),
        name="place",
    )(source, came0, came1, after)


def hold_kernel(*refs):
    pass


def hold_back(x, *after):
    spec = pl.BlockSpec(memory_space=pl.ANY)
    return pl.pallas_call(
        hold_kernel,
        in_specs=[spec] * (1 + len(after)),
        out_specs=spec,
        out_shape=jax.ShapeDtypeStruct(x.shape, x.dtype),
        input_output_aliases={0: 0},
        name="hold",
    )(x, *after)


def col_place(c):
    return c // 8, (c // 4) % 2, c % 4


def col_index(y, x, z):
    return (y % 4) * 8 + (x % 2) * 4 + z % 4


def col_shift(x, dy, dz):
    def to(c):
        py, px, pz = col_place(c)
        return col_index(py + dy, px, pz + dz)

    return lax.ppermute(x, "col", [(c, to(c)) for c in range(32)])


def ring_pieces(x, axis):
    step = (1, 0) if axis == "y" else (0, 1)
    back = (-step[0], -step[1])
    before = col_shift(x, *step)
    after = col_shift(x, *back)
    half = x.shape[0] // 2
    return [x, before, col_shift(before[:half], *step), col_shift(after[half:], *back), after]


def spots_for(col, first):
    offsets = (0, -1, -2, 1)
    py, px, pz = col_place(col)
    table = []
    for outer in offsets:
        for inner in offsets:
            for flip in range(2):
                dy, dz = (outer, inner) if first == "z" else (inner, outer)
                table.append(((py + dy) % 4) * 8 + (px ^ flip) * 4 + (pz + dz) % 4)
    return jnp.stack(table).astype(jnp.int32)


def gather_half(x, first):
    second = "y" if first == "z" else "z"
    return ring_pieces(jnp.concatenate(ring_pieces(x, first), axis=0), second)


def row_swap(x, k):
    return lax.ppermute(x, "row", [(r, r ^ k) for r in range(ROWS)])


def row_gather(x):
    near = row_swap(x, 2)
    return [x, near, row_swap(x, 1), row_swap(near, 1)]


def local(
    tokens,
    in_weight,
    out_weight,
    beta_weight,
    conv_weight,
    conv_prior,
    head_gain,
    state_pool,
    state_index,
    lengths,
    page_table,
):
    n_col = lax.axis_size("col")
    row_id = lax.axis_index("row")
    span = tokens.shape[1]
    heads = state_index.shape[1]
    prompts = lengths.shape[0]
    n_pages = prompts * PAGES_SEQ
    part = in_weight.shape[0]
    in_cols = in_weight.shape[1] // ROWS
    out_cols = out_weight.shape[1] // ROWS

    win = in_weight.astype(BF)
    wout = out_weight.astype(BF)
    half_in, half_out = in_cols // 2, out_cols // 2
    both = jnp.concatenate(
        [win.reshape(part, ROWS, 2, half_in), wout.reshape(part, ROWS, 2, half_out)], axis=3
    ).transpose(1, 0, 2, 3)
    both = both.reshape(ROWS, part, in_cols + out_cols)
    by_xor = [lax.dynamic_index_in_dim(both, row_id ^ k, 0, keepdims=False) for k in XORS]

    def swap(x, k, flip):
        pairs = [
            (r * 32 + c, (r ^ k) * 32 + (c ^ (4 * flip))) for r in range(ROWS) for c in range(32)
        ]
        return lax.ppermute(x, ("row", "col"), pairs)

    rows = [
        by_xor[i] if k == 0 and flip == 0 else swap(by_xor[i], k, flip)
        for flip in range(2)
        for i, k in enumerate(XORS)
    ]
    mine = jnp.concatenate(rows, axis=0).reshape(2, ROWS * part, in_cols + out_cols)
    cut = half_in + half_out
    halves = [gather_half(mine[:, :, :cut], "z"), gather_half(mine[:, :, cut:], "y")]
    col_id = lax.axis_index("col")
    spots = [spots_for(col_id, "z"), spots_for(col_id, "y")]
    toks = row_gather(tokens)

    targets = page_table[:, :, 0].reshape(-1)
    slots = page_table[:, :, 1].reshape(-1)
    beta = lax.dynamic_slice_in_dim(beta_weight, row_id * heads, heads, 1).astype(BF)
    beta = beta.reshape(ROWS, span, heads)
    beta = jnp.stack(
        [lax.dynamic_index_in_dim(beta, row_id ^ k, 0, keepdims=False) for k in XORS]
    )
    beta = jnp.pad(beta, ((0, 0), (0, 0), (0, DK - heads)))
    prior = jnp.pad(conv_prior.astype(F32), ((0, 0), (8 - (CONV - 1), 0), (0, 0)))

    q0, k0, v0, out0, rate = project(
        0, targets, lengths, spots[0], toks, halves[0], beta, conv_weight, prior, n_col,
        halves[1][1:],
    )
    came0 = lax.all_to_all(out0, "col", split_axis=0, concat_axis=0, tiled=True)
    states = state_index.reshape(-1)
    gain = head_gain.reshape(1, -1)
    normed0, state0 = scan_pair(0, lengths, states, q0, k0, v0, rate, gain, state_pool)
    q1, k1, v1, out1 = project(
        1, targets, lengths, spots[1], toks, halves[1], None, conv_weight, prior, n_col, [normed0]
    )
    heads0 = row_gather(normed0)
    normed1, final_state = scan_pair(
        1, lengths, states, q1, k1, v1, rate, gain, state_pool, state0
    )
    heads1 = row_gather(normed1)
    hit = targets[:, None] == jnp.arange(n_col, dtype=jnp.int32)[None, :]
    slot_for = jnp.max(jnp.where(hit, slots[:, None], -1), axis=0)
    block_in, block_out = win.shape[1] // n_col, wout.shape[1] // n_col
    send = jnp.concatenate(
        [
            win.reshape(part, n_col, block_in).transpose(1, 0, 2).reshape(n_col, -1, DK),
            wout.reshape(part, n_col, block_out).transpose(1, 0, 2).reshape(n_col, -1, DK),
            jnp.broadcast_to(slot_for.astype(BF)[:, None, None], (n_col, 8, DK)),
        ],
        axis=1,
    )
    send = hold_back(send, came0)
    got = lax.all_to_all(send, "col", split_axis=0, concat_axis=0, tiled=True)
    n_in = part * block_in // DK
    n_out = part * block_out // DK
    server_in = got[:, :n_in].reshape(n_col * part, block_in)
    server_out = got[:, n_in : n_in + n_out].reshape(n_col * part, block_out)
    arrived_slots = got[:, n_in + n_out, 0].astype(jnp.int32)
    wanted = arrived_slots[None, :] == jnp.arange(n_pages, dtype=jnp.int32)[:, None]
    source = jnp.sum(
        jnp.where(wanted, jnp.arange(n_col, dtype=jnp.int32)[None, :], 0), axis=1
    ).astype(jnp.int32)

    out1 = hold_back(out1, got, heads0[1], heads1[1])
    came1 = lax.all_to_all(out1, "col", split_axis=0, concat_axis=0, tiled=True)
    layer_out = out_product(
        jnp.stack(spots), heads0 + heads1, halves, half_in, half_out
    )
    page_cache = place_pages(source, came0, came1, n_pages, layer_out)
    return (server_in, server_out, layer_out, final_state, page_cache)


def solution(mesh):
    return jax.shard_map(
        local,
        mesh=mesh,
        in_specs=(
            P("col", "row"),
            P(("row", "col"), None),
            P(("row", "col"), None),
            P(),
            P(None, "row"),
            P("col", None, "row"),
            P("row"),
            P("col", "row", None, None),
            P("col", "row"),
            P("col"),
            P("col", None, None),
        ),
        out_specs=(
            P("row", "col"),
            P("row", "col"),
            P("col", "row"),
            P("col", "row", None, None),
            P("col", None, None, "row"),
        ),
        check_vma=False,
    )
```

time: 439 us -> 297 us (0.68)
  the two profiles are of different devices: /device:TPU:43 before, /device:TPU:16 now
where the time goes in v2:
time: 297 us; the launch traced here: 295 us
  waiting for transfers between devices  116 us (39%)
  Pallas kernels  84.6 us (28%)
  starting transfers between devices  58.3 us (20%)
  local copies, waits for them, and re-layouts  28.5 us (10%)
  other arithmetic  5.94 us (2%)
    ppermute x16, waiting for transfers between devices, col_shift(): return lax.ppermute(x, 'col', [(c, to(c)) for c in range(32)])  56.3 us
    pallas_call x2, Pallas kernels, project(): pl.pallas_call(functools.partial(proj_kernel, with_rate, len(pieces), len...  38.1 us
    pallas_call x2, Pallas kernels, scan_pair(): pl.pallas_call(functools.partial(scan_kernel, pair), grid_spec=grid_spec,...  30.7 us
    all_to_all x1, waiting for transfers between devices, local(): came1 = lax.all_to_all(out1, 'col', split_axis=0, concat_axis=0, tiled=True)  25.8 us
    ppermute x9, waiting for transfers between devices, row_swap(): return lax.ppermute(x, 'row', [(r, r ^ k) for r in range(ROWS)])  24.6 us
    ppermute x16, starting transfers between devices, col_shift(): return lax.ppermute(x, 'col', [(c, to(c)) for c in range(32)])  21.8 us
    unnamed x72, local copies, waits for them, and re-layouts  11.7 us
    ppermute x7, starting transfers between devices, swap(): return lax.ppermute(x, ('row', 'col'), pairs)  9.11 us
  transfers between devices with their start and end apart: 35, of which 19 were waited for; matrix products, arithmetic and copies ran while one was open for 8% of the time, Pallas kernels for 19%

profile of v2, /device:TPU:16, one launch (start us, length us, event | category | flops | bytes accessed | tf_op | source)
XLA Modules:
  0.0 294.5 jit_solution(3655618828809546344)
XLA Ops:
  4.5 3.1 %collective-permute-start.3 = (bf16[16,2048]{1,0:T(8,128)(2,1)S(1)}, bf16[16,2048]{1,0:T(8,128)(2,1)S(1)}, u32[]{:S(2)}, u32[]{:S(2)}) collective-permute-start(bf16[16,2048]{1,0:T(8,128)(2,1)S(1)} %bitcast.62), channel_id=1, source_target_pairs={{0,64},{1,65},{2,66},{3,67},{4,68},{5,69},{6,70},{7,71},{8,72},{9,... | collective-permute-start | bytes 196616 | tf_op jit(solution)/shard_map/ppermute | solution.py:433
  9.0 3.3 %collective-permute-start.5 = (bf16[16,2048]{1,0:T(8,128)(2,1)S(1)}, bf16[16,2048]{1,0:T(8,128)(2,1)S(1)}, u32[]{:S(2)}, u32[]{:S(2)}) collective-permute-start(bf16[16,2048]{1,0:T(8,128)(2,1)S(1)} %bitcast.66), channel_id=1, source_target_pairs={{0,96},{1,97},{2,98},{3,99},{4,100},{5,101},{6,102},{7,103},{8,104... | collective-permute-start | bytes 196616 | tf_op jit(solution)/shard_map/ppermute | solution.py:433
  13.8 1.9 collective-permute-done.5
  15.7 2.3 collective-permute-done.6
  21.1 6.0 %collective-permute-done.18 = bf16[2,64,1024]{2,1,0:T(8,128)(2,1)S(1)} collective-permute-done((bf16[2,64,1024]{2,1,0:T(8,128)(2,1)S(1)}, bf16[2,64,1024]{2,1,0:T(8,128)(2,1)S(1)}, u32[]{:S(2)}, u32[]{:S(2)}) %collective-permute-start.18) | collective-permute-done | bytes 262176 | tf_op jit(solution)/shard_map/ppermute | solution.py:359
  32.8 2.1 collective-permute-done.21
  36.2 1.9 collective-permute-start.22
  38.1 1.9 collective-permute-start.10
  41.4 25.2 %collective-permute-done.10 = bf16[2,64,1024]{2,1,0:T(8,128)(2,1)S(1)} collective-permute-done((bf16[2,64,1024]{2,1,0:T(8,128)(2,1)S(1)}, bf16[2,64,1024]{2,1,0:T(8,128)(2,1)S(1)}, u32[]{:S(2)}, u32[]{:S(2)}) %collective-permute-start.10) | collective-permute-done | bytes 262176 | tf_op jit(solution)/shard_map/ppermute | solution.py:359
  66.7 3.3 %collective-permute-start.13 = (bf16[1,64,1024]{2,1,0:T(8,128)(2,1)S(1)}, bf16[1,64,1024]{2,1,0:T(8,128)(2,1)S(1)}, u32[]{:S(2)}, u32[]{:S(2)}) collective-permute-start(bf16[1,64,1024]{2,1,0:T(8,128)(2,1)S(1)} %slice.62), channel_id=1, source_target_pairs={{0,3},{1,0},{2,1},{3,2},{4,7},{5,4},{6,5},{7,6},{8,11},{9,8},{10,9... | collective-permute-start | bytes 393224 | tf_op jit(solution)/shard_map/ppermute | solution.py:359
  70.7 2.1 collective-permute-done.11
  76.3 2.7 collective-permute-start.14
  80.2 14.9 %collective-permute-done.24.refs_15_.refs_8_.refs_17_ = bf16[8,64,1024]{2,1,0:T(8,128)(2,1)S(1)} collective-permute-done((bf16[8,64,1024]{2,1,0:T(8,128)(2,1)}, bf16[8,64,1024]{2,1,0:T(8,128)(2,1)S(1)}, u32[]{:S(2)}, u32[]{:S(2)}) %collective-permute-start.24) | collective-permute-done | bytes 1048608 | tf_op jit(solution)/shard_map/ppermute | solution.py:359
  96.7 2.5 collective-permute-start.25
  101.1 2.5 collective-permute-start.15
  103.6 1.9 slice.64
  107.2 1.9 pad.10.refs_9_
  110.6 4.4 %collective-permute-done.17.refs_7_.refs_11_ = bf16[4,64,1024]{2,1,0:T(8,128)(2,1)} collective-permute-done((bf16[4,64,1024]{2,1,0:T(8,128)(2,1)}, bf16[4,64,1024]{2,1,0:T(8,128)(2,1)}, u32[]{:S(2)}, u32[]{:S(2)}) %collective-permute-start.17) | collective-permute-done | bytes 524320 | tf_op jit(solution)/shard_map/ppermute | solution.py:359
  115.0 20.1 %project.2 = (bf16[2,1536,128]{2,1,0:T(8,128)(2,1)}, bf16[2,1536,128]{2,1,0:T(8,128)(2,1)}, bf16[2,1536,128]{2,1,0:T(8,128)(2,1)}, bf16[32,256,256]{2,1,0:T(8,128)(2,1)}, f32[1536,128]{1,0:T(8,128)}) custom-call(s32[12]{0:T(128)} %eq.163.targets, s32[3]{0:T(128)} %lens.7, s32[32]{0:T(128)} %stack.182.spots, bf16[1536,512]{1,0:T(8,128)(2,1)} %refs_0_.3, ...), custom_call_target="tpu_custom_call" | custom-call | flops 4831838208 | bytes 14680064 | tf_op jit(solution)/shard_map/project/pallas_call | solution.py:139
  135.1 6.1 %all-to-all-start = ((bf16[32,256,256]{2,1,0:T(8,128)(2,1)}), bf16[32,256,256]{2,1,0:T(8,128)(2,1)}, u32[]{:S(2)}, u32[]{:S(2)}) async-start(bf16[32,256,256]{2,1,0:T(8,128)(2,1)} %get-tuple-element.18), calls=%async_computation | async-start | bytes 8388608 | tf_op jit(solution)/shard_map/all_to_all | solution.py:461
  142.6 15.3 %delta.2 = (bf16[1536,256]{1,0:T(8,128)(2,1)}, f32[3,4,128,128]{3,2,1,0:T(8,128)}) custom-call(s32[3]{0:T(128)} %lens.7, s32[12]{0:T(128)} %reshape.72.index, bf16[2,1536,128]{2,1,0:T(8,128)(2,1)} %get-tuple-element.19.q_ref, bf16[2,1536,128]{2,1,0:T(8,128)(2,1)} %get-tuple-element.20.k_ref, bf16[2,1536,128]{2,1,0:T(8,128)(2,1)} %get-tuple-element.21.v_ref, ...), custom_call_target="tpu_custom_call" | custom-call | flops 12884901888 | bytes 6291456 | tf_op jit(solution)/shard_map/delta/pallas_call | solution.py:245
  157.9 18.0 %project.3 = (bf16[2,1536,128]{2,1,0:T(8,128)(2,1)}, bf16[2,1536,128]{2,1,0:T(8,128)(2,1)}, bf16[2,1536,128]{2,1,0:T(8,128)(2,1)}, bf16[32,256,256]{2,1,0:T(8,128)(2,1)}) custom-call(s32[12]{0:T(128)} %eq.163.targets, s32[3]{0:T(128)} %lens.7, s32[32]{0:T(128)} %stack.185.spots, bf16[1536,512]{1,0:T(8,128)(2,1)} %refs_0_.3, ...), custom_call_target="tpu_custom_call" | custom-call | flops 4831838208 | bytes 14680064 | tf_op jit(solution)/shard_map/project/pallas_call | solution.py:139
  175.9 15.4 %delta.3 = (bf16[1536,256]{1,0:T(8,128)(2,1)}, f32[3,4,128,128]{3,2,1,0:T(8,128)}) custom-call(s32[3]{0:T(128)} %lens.7, s32[12]{0:T(128)} %reshape.72.index, bf16[2,1536,128]{2,1,0:T(8,128)(2,1)} %get-tuple-element.24.q_ref, bf16[2,1536,128]{2,1,0:T(8,128)(2,1)} %get-tuple-element.25.k_ref, ...), custom_call_target="tpu_custom_call", output_to_operand_aliasing={{1}: (8, {})} | custom-call | flops 12884901888 | bytes 6291456 | tf_op jit(solution)/shard_map/delta/pallas_call | solution.py:245
  191.3 3.8 %collective-permute-start.29 = (bf16[1536,256]{1,0:T(8,128)(2,1)}, bf16[1536,256]{1,0:T(8,128)(2,1)S(1)}, u32[]{:S(2)}, u32[]{:S(2)}) collective-permute-start(bf16[1536,256]{1,0:T(8,128)(2,1)} %get-tuple-element.28.refs_4_), channel_id=1, source_target_pairs={{0,64},{32,96},{64,0},{96,32},{1,65},{33,97},{65,1},{97,33},{2,66}... | collective-permute-start | bytes 2359304 | tf_op jit(solution)/shard_map/ppermute | solution.py:389
  197.5 7.9 %all-to-all-start.1 = ((bf16[32,40,128]{2,1,0:T(8,128)(2,1)}), bf16[32,40,128]{2,1,0:T(8,128)(2,1)S(1)}, u32[]{:S(2)}, u32[]{:S(2)}) async-start(bf16[32,40,128]{2,1,0:T(8,128)(2,1)} %hold.2), calls=%async_computation.1 | async-start | bytes 655360 | tf_op jit(solution)/shard_map/all_to_all | solution.py:485
  205.4 8.4 %collective-permute-done.29.refs_5_.refs_3_ = bf16[1536,256]{1,0:T(8,128)(2,1)S(1)} collective-permute-done((bf16[1536,256]{1,0:T(8,128)(2,1)}, bf16[1536,256]{1,0:T(8,128)(2,1)S(1)}, u32[]{:S(2)}, u32[]{:S(2)}) %collective-permute-start.29) | collective-permute-done | bytes 786464 | tf_op jit(solution)/shard_map/ppermute | solution.py:389
  213.8 11.5 %collective-permute-done.26.refs_1_.refs_2_ = bf16[1536,256]{1,0:T(8,128)(2,1)S(1)} collective-permute-done((bf16[1536,256]{1,0:T(8,128)(2,1)S(1)}, bf16[1536,256]{1,0:T(8,128)(2,1)S(1)}, u32[]{:S(2)}, u32[]{:S(2)}) %collective-permute-start.26) | collective-permute-done | bytes 786464 | tf_op jit(solution)/shard_map/ppermute | solution.py:389
  225.4 5.0 %all-to-all-done.1.refs_1_ = bf16[32,40,128]{2,1,0:T(8,128)(2,1)S(1)} async-done(((bf16[32,40,128]{2,1,0:T(8,128)(2,1)}), bf16[32,40,128]{2,1,0:T(8,128)(2,1)S(1)}, u32[]{:S(2)}, u32[]{:S(2)}) %all-to-all-start.1) | async-done | bytes 327712 | tf_op jit(solution)/shard_map/all_to_all | solution.py:485
  231.1 6.8 %all-to-all-start.2 = ((bf16[32,256,256]{2,1,0:T(8,128)(2,1)}), bf16[32,256,256]{2,1,0:T(8,128)(2,1)}, u32[]{:S(2)}, u32[]{:S(2)}) async-start(bf16[32,256,256]{2,1,0:T(8,128)(2,1)} %hold.3), calls=%async_computation.2 | async-start | bytes 8388608 | tf_op jit(solution)/shard_map/all_to_all | solution.py:497
  248.1 6.7 %outmix.1.after = bf16[1536,512]{1,0:T(8,128)(2,1)} custom-call(s32[2,32]{1,0:T(2,128)S(1)} %pad_add_fusion.spots, bf16[1536,256]{1,0:T(8,128)(2,1)S(1)} %copy-done.9, bf16[1536,256]{1,0:T(8,128)(2,1)S(1)} %copy-done.4, bf16[1536,256]{1,0:T(8,128)(2,1)S(1)} %collective-permute-done.27.refs_2_, bf16[1536,256]{1,0:T(8,128)(2,1)S(1)} %collective-permute-done.28.refs_3_, ...), custom_call_target="tpu_custom_call" | custom-call | flops 3221225472 | bytes 10485760 | tf_op jit(solution)/shard_map/outmix/pallas_call | solution.py:294
  259.6 25.8 %all-to-all-done.2.x1 = bf16[32,256,256]{2,1,0:T(8,128)(2,1)} async-done(((bf16[32,256,256]{2,1,0:T(8,128)(2,1)}), bf16[32,256,256]{2,1,0:T(8,128)(2,1)}, u32[]{:S(2)}, u32[]{:S(2)}) %all-to-all-start.2) | async-done | bytes 4194336 | tf_op jit(solution)/shard_map/all_to_all | solution.py:497
  285.4 9.1 %place.1 = bf16[12,128,2,512]{3,2,1,0:T(2,128)(2,1)} custom-call(s32[12]{0:T(128)} %select_reduce_fusion.source, bf16[32,256,256]{2,1,0:T(8,128)(2,1)} %all-to-all-done.refs_1_.x0, bf16[32,256,256]{2,1,0:T(8,128)(2,1)} %all-to-all-done.2.x1, bf16[1536,512]{1,0:T(8,128)(2,1)} %outmix.1.after), custom_call_target="tpu_custom_call" | custom-call | bytes 6291456 | tf_op jit(solution)/shard_map/place/pallas_call | solution.py:321
  (166 shorter events, 49.0 us)
Async XLA Ops:
  4.5 7.9 %collective-permute-start.3 = (bf16[16,2048]{1,0:T(8,128)(2,1)S(1)}, bf16[16,2048]{1,0:T(8,128)(2,1)S(1)}, u32[]{:S(2)}, u32[]{:S(2)}) collective-permute-start(bf16[16,2048]{1,0:T(8,128)(2,1)S(1)} %bitcast.62), channel_id=1, source_target_pairs={{0,64},{1,65},{2,66},{3,67},{4,68},{5,69},{6,70},{7,71},{8,72},{9,... | collective-permute-start | bytes 196616 | tf_op jit(solution)/shard_map/ppermute | solution.py:433
  7.6 10.5 %collective-permute-start.7 = (bf16[16,2048]{1,0:T(8,128)(2,1)S(1)}, bf16[16,2048]{1,0:T(8,128)(2,1)S(1)}, u32[]{:S(2)}, u32[]{:S(2)}) collective-permute-start(bf16[16,2048]{1,0:T(8,128)(2,1)S(1)} %bitcast.63), channel_id=1, source_target_pairs={{0,68},{1,69},{2,70},{3,71},{4,64},{5,65},{6,66},{7,67},{8,76},{9,... | collective-permute-start | bytes 196616 | tf_op jit(solution)/shard_map/ppermute | solution.py:433
  8.8 4.9 %collective-permute-start.4 = (bf16[16,2048]{1,0:T(8,128)(2,1)S(1)}, bf16[16,2048]{1,0:T(8,128)(2,1)S(1)}, u32[]{:S(2)}, u32[]{:S(2)}) collective-permute-start(bf16[16,2048]{1,0:T(8,128)(2,1)S(1)} %bitcast.64), channel_id=1, source_target_pairs={{0,32},{1,33},{2,34},{3,35},{4,36},{5,37},{6,38},{7,39},{8,40},{9,... | collective-permute-start | bytes 196616 | tf_op jit(solution)/shard_map/ppermute | solution.py:433
  8.9 9.2 %collective-permute-start.8 = (bf16[16,2048]{1,0:T(8,128)(2,1)S(1)}, bf16[16,2048]{1,0:T(8,128)(2,1)S(1)}, u32[]{:S(2)}, u32[]{:S(2)}) collective-permute-start(bf16[16,2048]{1,0:T(8,128)(2,1)S(1)} %bitcast.65), channel_id=1, source_target_pairs={{0,36},{1,37},{2,38},{3,39},{4,32},{5,33},{6,34},{7,35},{8,44},{9,... | collective-permute-start | bytes 196616 | tf_op jit(solution)/shard_map/ppermute | solution.py:433
  9.0 6.7 %collective-permute-start.5 = (bf16[16,2048]{1,0:T(8,128)(2,1)S(1)}, bf16[16,2048]{1,0:T(8,128)(2,1)S(1)}, u32[]{:S(2)}, u32[]{:S(2)}) collective-permute-start(bf16[16,2048]{1,0:T(8,128)(2,1)S(1)} %bitcast.66), channel_id=1, source_target_pairs={{0,96},{1,97},{2,98},{3,99},{4,100},{5,101},{6,102},{7,103},{8,104... | collective-permute-start | bytes 196616 | tf_op jit(solution)/shard_map/ppermute | solution.py:433
  12.4 5.7 %collective-permute-start.9 = (bf16[16,2048]{1,0:T(8,128)(2,1)S(1)}, bf16[16,2048]{1,0:T(8,128)(2,1)S(1)}, u32[]{:S(2)}, u32[]{:S(2)}) collective-permute-start(bf16[16,2048]{1,0:T(8,128)(2,1)S(1)} %bitcast.67), channel_id=1, source_target_pairs={{0,100},{1,101},{2,102},{3,103},{4,96},{5,97},{6,98},{7,99},{8,108... | collective-permute-start | bytes 196616 | tf_op jit(solution)/shard_map/ppermute | solution.py:433
  13.7 4.3 %collective-permute-start.6 = (bf16[16,2048]{1,0:T(8,128)(2,1)S(1)}, bf16[16,2048]{1,0:T(8,128)(2,1)S(1)}, u32[]{:S(2)}, u32[]{:S(2)}) collective-permute-start(bf16[16,2048]{1,0:T(8,128)(2,1)S(1)} %get-tuple-element.54), channel_id=1, source_target_pairs={{0,4},{1,5},{2,6},{3,7},{4,0},{5,1},{6,2},{7,3},{8,12},{9,13},{10,... | collective-permute-start | bytes 196616 | tf_op jit(solution)/shard_map/ppermute | solution.py:433
  19.0 8.0 %collective-permute-start.18 = (bf16[2,64,1024]{2,1,0:T(8,128)(2,1)S(1)}, bf16[2,64,1024]{2,1,0:T(8,128)(2,1)S(1)}, u32[]{:S(2)}, u32[]{:S(2)}) collective-permute-start(bf16[2,64,1024]{2,1,0:T(8,128)(2,1)S(1)} %get-tuple-element.55), channel_id=1, source_target_pairs={{0,8},{1,9},{2,10},{3,11},{4,12},{5,13},{6,14},{7,15},{8,16},{9,17... | collective-permute-start | bytes 786440 | tf_op jit(solution)/shard_map/ppermute | solution.py:359
  20.3 9.5 %collective-permute-start.20 = (bf16[2,64,1024]{2,1,0:T(8,128)(2,1)S(1)}, bf16[2,64,1024]{2,1,0:T(8,128)(2,1)S(1)}, u32[]{:S(2)}, u32[]{:S(2)}) collective-permute-start(bf16[2,64,1024]{2,1,0:T(8,128)(2,1)S(1)} %get-tuple-element.55), channel_id=1, source_target_pairs={{0,24},{1,25},{2,26},{3,27},{4,28},{5,29},{6,30},{7,31},{8,0},{9,1... | collective-permute-start | bytes 786440 | tf_op jit(solution)/shard_map/ppermute | solution.py:359
  27.1 5.0 %collective-permute-start.19 = (bf16[1,64,1024]{2,1,0:T(8,128)(2,1)S(1)}, bf16[1,64,1024]{2,1,0:T(8,128)(2,1)S(1)}, u32[]{:S(2)}, u32[]{:S(2)}) collective-permute-start(bf16[1,64,1024]{2,1,0:T(8,128)(2,1)S(1)} %slice.66), channel_id=1, source_target_pairs={{0,8},{1,9},{2,10},{3,11},{4,12},{5,13},{6,14},{7,15},{8,16},{9,17... | collective-permute-start | bytes 393224 | tf_op jit(solution)/shard_map/ppermute | solution.py:359
  28.4 50.6 %collective-permute-start = (bf16[1536,512]{1,0:T(8,128)(2,1)}, bf16[1536,512]{1,0:T(8,128)(2,1)}, u32[]{:S(2)}, u32[]{:S(2)}) collective-permute-start(bf16[1536,512]{1,0:T(8,128)(2,1)} %refs_0_.3), channel_id=1, source_target_pairs={{0,64},{32,96},{64,0},{96,32},{1,65},{33,97},{65,1},{97,33},{2,66}... | collective-permute-start | bytes 4718600 | tf_op jit(solution)/shard_map/ppermute | solution.py:389
  29.8 5.0 %collective-permute-start.21 = (bf16[1,64,1024]{2,1,0:T(8,128)(2,1)S(1)}, bf16[1,64,1024]{2,1,0:T(8,128)(2,1)S(1)}, u32[]{:S(2)}, u32[]{:S(2)}) collective-permute-start(bf16[1,64,1024]{2,1,0:T(8,128)(2,1)S(1)} %slice.67), channel_id=1, source_target_pairs={{0,24},{1,25},{2,26},{3,27},{4,28},{5,29},{6,30},{7,31},{8,0},{9,1... | collective-permute-start | bytes 393224 | tf_op jit(solution)/shard_map/ppermute | solution.py:359
  36.2 42.8 %collective-permute-start.22 = (bf16[8,64,1024]{2,1,0:T(8,128)(2,1)}, bf16[8,64,1024]{2,1,0:T(8,128)(2,1)S(1)}, u32[]{:S(2)}, u32[]{:S(2)}) collective-permute-start(bf16[8,64,1024]{2,1,0:T(8,128)(2,1)} %constant_dynamic-update-slice_fusion.13.refs_4_.refs_13_), channel_id=1, source_target_pairs={{0,1},{1,2},{2,3},{3,0},{4,5},{5,6},{6,7},{7,4},{8,9},{9,10},{10,1... | collective-permute-start | bytes 3145736 | tf_op jit(solution)/shard_map/ppermute | solution.py:359
  38.1 28.5 %collective-permute-start.10 = (bf16[2,64,1024]{2,1,0:T(8,128)(2,1)S(1)}, bf16[2,64,1024]{2,1,0:T(8,128)(2,1)S(1)}, u32[]{:S(2)}, u32[]{:S(2)}) collective-permute-start(bf16[2,64,1024]{2,1,0:T(8,128)(2,1)S(1)} %get-tuple-element.58), channel_id=1, source_target_pairs={{0,1},{1,2},{2,3},{3,0},{4,5},{5,6},{6,7},{7,4},{8,9},{9,10},{10,1... | collective-permute-start | bytes 786440 | tf_op jit(solution)/shard_map/ppermute | solution.py:359
  40.1 26.7 %collective-permute-start.12 = (bf16[2,64,1024]{2,1,0:T(8,128)(2,1)S(1)}, bf16[2,64,1024]{2,1,0:T(8,128)(2,1)S(1)}, u32[]{:S(2)}, u32[]{:S(2)}) collective-permute-start(bf16[2,64,1024]{2,1,0:T(8,128)(2,1)S(1)} %get-tuple-element.58), channel_id=1, source_target_pairs={{0,3},{1,0},{2,1},{3,2},{4,7},{5,4},{6,5},{7,6},{8,11},{9,8},{10,9... | collective-permute-start | bytes 786440 | tf_op jit(solution)/shard_map/ppermute | solution.py:359
  41.4 64.1 %collective-permute-start.1 = (bf16[1536,512]{1,0:T(8,128)(2,1)}, bf16[1536,512]{1,0:T(8,128)(2,1)}, u32[]{:S(2)}, u32[]{:S(2)}) collective-permute-start(bf16[1536,512]{1,0:T(8,128)(2,1)} %refs_0_.3), channel_id=1, source_target_pairs={{0,32},{32,0},{64,96},{96,64},{1,33},{33,1},{65,97},{97,65},{2,34}... | collective-permute-start | bytes 4718600 | tf_op jit(solution)/shard_map/ppermute | solution.py:389
  66.6 6.2 %collective-permute-start.11 = (bf16[1,64,1024]{2,1,0:T(8,128)(2,1)S(1)}, bf16[1,64,1024]{2,1,0:T(8,128)(2,1)S(1)}, u32[]{:S(2)}, u32[]{:S(2)}) collective-permute-start(bf16[1,64,1024]{2,1,0:T(8,128)(2,1)S(1)} %slice.61), channel_id=1, source_target_pairs={{0,1},{1,2},{2,3},{3,0},{4,5},{5,6},{6,7},{7,4},{8,9},{9,10},{10,1... | collective-permute-start | bytes 393224 | tf_op jit(solution)/shard_map/ppermute | solution.py:359
  66.7 8.2 %collective-permute-start.13 = (bf16[1,64,1024]{2,1,0:T(8,128)(2,1)S(1)}, bf16[1,64,1024]{2,1,0:T(8,128)(2,1)S(1)}, u32[]{:S(2)}, u32[]{:S(2)}) collective-permute-start(bf16[1,64,1024]{2,1,0:T(8,128)(2,1)S(1)} %slice.62), channel_id=1, source_target_pairs={{0,3},{1,0},{2,1},{3,2},{4,7},{5,4},{6,5},{7,6},{8,11},{9,8},{10,9... | collective-permute-start | bytes 393224 | tf_op jit(solution)/shard_map/ppermute | solution.py:359
  72.9 22.3 %collective-permute-start.24 = (bf16[8,64,1024]{2,1,0:T(8,128)(2,1)}, bf16[8,64,1024]{2,1,0:T(8,128)(2,1)S(1)}, u32[]{:S(2)}, u32[]{:S(2)}) collective-permute-start(bf16[8,64,1024]{2,1,0:T(8,128)(2,1)} %constant_dynamic-update-slice_fusion.13.refs_4_.refs_13_), channel_id=1, source_target_pairs={{0,3},{1,0},{2,1},{3,2},{4,7},{5,4},{6,5},{7,6},{8,11},{9,8},{10,9... | collective-permute-start | bytes 3145736 | tf_op jit(solution)/shard_map/ppermute | solution.py:359
  76.3 20.4 %collective-permute-start.14 = (bf16[8,64,1024]{2,1,0:T(8,128)(2,1)}, bf16[8,64,1024]{2,1,0:T(8,128)(2,1)}, u32[]{:S(2)}, u32[]{:S(2)}) collective-permute-start(bf16[8,64,1024]{2,1,0:T(8,128)(2,1)} %constant_dynamic-update-slice_fusion.8.refs_4_.refs_8_), channel_id=1, source_target_pairs={{0,8},{1,9},{2,10},{3,11},{4,12},{5,13},{6,14},{7,15},{8,16},{9,17... | collective-permute-start | bytes 3145736 | tf_op jit(solution)/shard_map/ppermute | solution.py:359
  79.0 22.1 %collective-permute-start.16 = (bf16[8,64,1024]{2,1,0:T(8,128)(2,1)}, bf16[8,64,1024]{2,1,0:T(8,128)(2,1)}, u32[]{:S(2)}, u32[]{:S(2)}) collective-permute-start(bf16[8,64,1024]{2,1,0:T(8,128)(2,1)} %constant_dynamic-update-slice_fusion.8.refs_4_.refs_8_), channel_id=1, source_target_pairs={{0,24},{1,25},{2,26},{3,27},{4,28},{5,29},{6,30},{7,31},{8,0},{9,1... | collective-permute-start | bytes 3145736 | tf_op jit(solution)/shard_map/ppermute | solution.py:359
  79.0 36.0 %collective-permute-start.2 = (bf16[1536,512]{1,0:T(8,128)(2,1)}, bf16[1536,512]{1,0:T(8,128)(2,1)}, u32[]{:S(2)}, u32[]{:S(2)}) collective-permute-start(bf16[1536,512]{1,0:T(8,128)(2,1)} %collective-permute-done.refs_1_), channel_id=1, source_target_pairs={{0,32},{32,0},{64,96},{96,64},{1,33},{33,1},{65,97},{97,65},{2,34}... | collective-permute-start | bytes 4718600 | tf_op jit(solution)/shard_map/ppermute | solution.py:389
  95.2 15.3 %collective-permute-start.23 = (bf16[4,64,1024]{2,1,0:T(8,128)(2,1)}, bf16[4,64,1024]{2,1,0:T(8,128)(2,1)S(1)}, u32[]{:S(2)}, u32[]{:S(2)}) collective-permute-start(bf16[4,64,1024]{2,1,0:T(8,128)(2,1)} %slice.68), channel_id=1, source_target_pairs={{0,1},{1,2},{2,3},{3,0},{4,5},{5,6},{6,7},{7,4},{8,9},{9,10},{10,1... | collective-permute-start | bytes 1572872 | tf_op jit(solution)/shard_map/ppermute | solution.py:359
  96.7 13.8 %collective-permute-start.25 = (bf16[4,64,1024]{2,1,0:T(8,128)(2,1)}, bf16[4,64,1024]{2,1,0:T(8,128)(2,1)S(1)}, u32[]{:S(2)}, u32[]{:S(2)}) collective-permute-start(bf16[4,64,1024]{2,1,0:T(8,128)(2,1)} %slice.69), channel_id=1, source_target_pairs={{0,3},{1,0},{2,1},{3,2},{4,7},{5,4},{6,5},{7,6},{8,11},{9,8},{10,9... | collective-permute-start | bytes 1572872 | tf_op jit(solution)/shard_map/ppermute | solution.py:359
  101.1 9.5 %collective-permute-start.15 = (bf16[4,64,1024]{2,1,0:T(8,128)(2,1)}, bf16[4,64,1024]{2,1,0:T(8,128)(2,1)}, u32[]{:S(2)}, u32[]{:S(2)}) collective-permute-start(bf16[4,64,1024]{2,1,0:T(8,128)(2,1)} %slice.63), channel_id=1, source_target_pairs={{0,8},{1,9},{2,10},{3,11},{4,12},{5,13},{6,14},{7,15},{8,16},{9,17... | collective-permute-start | bytes 1572872 | tf_op jit(solution)/shard_map/ppermute | solution.py:359
  105.5 9.5 %collective-permute-start.17 = (bf16[4,64,1024]{2,1,0:T(8,128)(2,1)}, bf16[4,64,1024]{2,1,0:T(8,128)(2,1)}, u32[]{:S(2)}, u32[]{:S(2)}) collective-permute-start(bf16[4,64,1024]{2,1,0:T(8,128)(2,1)} %slice.64), channel_id=1, source_target_pairs={{0,24},{1,25},{2,26},{3,27},{4,28},{5,29},{6,30},{7,31},{8,0},{9,1... | collective-permute-start | bytes 1572872 | tf_op jit(solution)/shard_map/ppermute | solution.py:359
  135.1 62.3 %all-to-all-start = ((bf16[32,256,256]{2,1,0:T(8,128)(2,1)}), bf16[32,256,256]{2,1,0:T(8,128)(2,1)}, u32[]{:S(2)}, u32[]{:S(2)}) async-start(bf16[32,256,256]{2,1,0:T(8,128)(2,1)} %get-tuple-element.18), calls=%async_computation | async-start | bytes 8388608 | tf_op jit(solution)/shard_map/all_to_all | solution.py:461
  191.3 22.5 %collective-permute-start.29 = (bf16[1536,256]{1,0:T(8,128)(2,1)}, bf16[1536,256]{1,0:T(8,128)(2,1)S(1)}, u32[]{:S(2)}, u32[]{:S(2)}) collective-permute-start(bf16[1536,256]{1,0:T(8,128)(2,1)} %get-tuple-element.28.refs_4_), channel_id=1, source_target_pairs={{0,64},{32,96},{64,0},{96,32},{1,65},{33,97},{65,1},{97,33},{2,66}... | collective-permute-start | bytes 2359304 | tf_op jit(solution)/shard_map/ppermute | solution.py:389
  195.2 30.2 %collective-permute-start.26 = (bf16[1536,256]{1,0:T(8,128)(2,1)S(1)}, bf16[1536,256]{1,0:T(8,128)(2,1)S(1)}, u32[]{:S(2)}, u32[]{:S(2)}) collective-permute-start(bf16[1536,256]{1,0:T(8,128)(2,1)S(1)} %copy-done.9), channel_id=1, source_target_pairs={{0,64},{32,96},{64,0},{96,32},{1,65},{33,97},{65,1},{97,33},{2,66}... | collective-permute-start | bytes 2359304 | tf_op jit(solution)/shard_map/ppermute | solution.py:389
  197.5 32.8 %all-to-all-start.1 = ((bf16[32,40,128]{2,1,0:T(8,128)(2,1)}), bf16[32,40,128]{2,1,0:T(8,128)(2,1)S(1)}, u32[]{:S(2)}, u32[]{:S(2)}) async-start(bf16[32,40,128]{2,1,0:T(8,128)(2,1)} %hold.2), calls=%async_computation.1 | async-start | bytes 655360 | tf_op jit(solution)/shard_map/all_to_all | solution.py:485
  231.1 54.3 %all-to-all-start.2 = ((bf16[32,256,256]{2,1,0:T(8,128)(2,1)}), bf16[32,256,256]{2,1,0:T(8,128)(2,1)}, u32[]{:S(2)}, u32[]{:S(2)}) async-start(bf16[32,256,256]{2,1,0:T(8,128)(2,1)} %hold.3), calls=%async_computation.2 | async-start | bytes 8388608 | tf_op jit(solution)/shard_map/all_to_all | solution.py:497
  238.6 5.1 %collective-permute-start.28 = (bf16[1536,256]{1,0:T(8,128)(2,1)S(1)}, bf16[1536,256]{1,0:T(8,128)(2,1)S(1)}, u32[]{:S(2)}, u32[]{:S(2)}) collective-permute-start(bf16[1536,256]{1,0:T(8,128)(2,1)S(1)} %copy-done.4), channel_id=1, source_target_pairs={{0,32},{32,0},{64,96},{96,64},{1,33},{33,1},{65,97},{97,65},{2,34}... | collective-permute-start | bytes 2359304 | tf_op jit(solution)/shard_map/ppermute | solution.py:389
  (30 other events, 378.1 us)
